TPU v7x, 32 devices: a whole 2x2x4 slice. The times are simulated.
32 devices in a mesh: expert: 4 (over z), fsdp: 8 (over y, x, core).
Axes of the slice: x: 2, y: 2, z: 4, core: 2. Of those that a mesh axis runs over, the one named last changes fastest.
Arguments:
- tokens: bfloat16 [8192, 2048], P(('expert', 'fsdp')), may hold values from -6 to 6
- expert_ids: int32 [8192, 6], P(('expert', 'fsdp')), may hold values from 0 to 63, as said below
- gate_vals: bfloat16 [8192, 6], P(('expert', 'fsdp')), may hold values from 0.099609375 to 1
- w_gate: bfloat16 [4, 2048, 1408], P('expert', 'fsdp'), may hold values from -0.125 to 0.125
- w_up: bfloat16 [4, 2048, 1408], P('expert', 'fsdp'), may hold values from -0.125 to 0.125
- w_down: bfloat16 [4, 2048, 1408], P('expert', 'fsdp'), may hold values from -0.15625 to 0.15625
- cotangent: bfloat16 [8192, 2048], P(('expert', 'fsdp')), may hold values from -6 to 6
Outputs:
- output: bfloat16 [8192, 2048], P(('expert', 'fsdp'))
- grad_tokens: bfloat16 [8192, 2048], P(('expert', 'fsdp'))
- grad_gates: float32 [8192, 6], P(('expert', 'fsdp'))
- grad_w_gate: float32 [4, 2048, 1408], P('expert', 'fsdp')
- grad_w_up: float32 [4, 2048, 1408], P('expert', 'fsdp')
- grad_w_down: float32 [4, 2048, 1408], P('expert', 'fsdp')
Inputs may be any that keep to these rules, and one draw needn't show every extreme that they name: `expert_ids`: each row names 6 different experts. Among the tokens of one device at most 48 name any one expert whose number modulo 16 is below 1. On every device some such expert is named by exactly 48 of its tokens, and for every column one such expert is named by exactly 48 tokens of every device of that column.
All inputs are finite; a program needn't handle non-finite values.
Results may differ from a plain program's by a relative error of at most 0.013.
Values may be sent and summed in bfloat16 or wider, within the bound.
A program may use at most 128 MiB of HBM per device.

v0:
```python
import jax
import jax.numpy as jnp
from jax import lax
from jax.sharding import PartitionSpec as P

EXPERTS = 64
TOP = 6
WAVE = 1
MOST = 48


def slot_tables(expert_ids, groups):
    per_index = EXPERTS // groups
    window = WAVE * groups
    tok_count = expert_ids.shape[0]
    flat_ids = expert_ids.reshape(-1)
    local_index = flat_ids % per_index
    is_live = local_index < WAVE
    window_slot = jnp.where(is_live, flat_ids // per_index * WAVE + local_index, window)
    onehot = (window_slot[:, None] == jnp.arange(window, dtype=jnp.int32)[None, :]).astype(
        jnp.int32
    )
    rank_in = jnp.sum((jnp.cumsum(onehot, axis=0) - 1) * onehot, axis=1)
    target = jnp.where(is_live, window_slot * MOST + rank_in, window * MOST)
    slot_ids = jnp.arange(tok_count * TOP, dtype=jnp.int32)
    source = (
        jnp.full((window * MOST,), tok_count * TOP, jnp.int32).at[target].set(slot_ids, mode="drop")
    )
    return (target, source)


def on_device(tokens, expert_ids, gate_vals, w_gate, w_up, w_down, cotangent):
    groups = lax.axis_size("expert")
    tok_count, model_width = tokens.shape
    target, source = slot_tables(expert_ids, groups)
    token_of = source // TOP
    zero_row = jnp.zeros((1, model_width), jnp.bfloat16)
    tokens_pad = jnp.concatenate([tokens, zero_row], axis=0)
    cot_pad = jnp.concatenate([cotangent, zero_row], axis=0)
    gate_pad = jnp.concatenate([gate_vals.reshape(-1), jnp.zeros((1,), jnp.bfloat16)], axis=0)
    send_rows = tokens_pad[token_of].reshape(groups, WAVE * MOST, model_width)
    arrived = lax.all_to_all(send_rows, "expert", split_axis=0, concat_axis=0, tiled=True)
    rows_in = arrived.reshape(groups, WAVE, MOST, model_width)
    full_gate, full_up, full_down = (
        lax.all_gather(w_gate, "fsdp", axis=1, tiled=True),
        lax.all_gather(w_up, "fsdp", axis=1, tiled=True),
        lax.all_gather(w_down, "fsdp", axis=1, tiled=True),
    )
    gate_pre = jnp.einsum("skmd,kdf->skmf", rows_in, full_gate, preferred_element_type=jnp.float32)
    up_pre = jnp.einsum("skmd,kdf->skmf", rows_in, full_up, preferred_element_type=jnp.float32)
    sigmoid_g = jax.nn.sigmoid(gate_pre)
    hidden = (gate_pre * sigmoid_g * up_pre).astype(jnp.bfloat16)
    expert_out = jnp.einsum(
        "skmf,kdf->skmd", hidden, full_down, preferred_element_type=jnp.float32
    ).astype(jnp.bfloat16)
    returned = lax.all_to_all(
        expert_out.reshape(groups, WAVE * MOST, model_width),
        "expert",
        split_axis=0,
        concat_axis=0,
        tiled=True,
    )
    back_pad = jnp.concatenate([returned.reshape(-1, model_width), zero_row], axis=0)
    slot_out = back_pad[target].reshape(tok_count, TOP, model_width).astype(jnp.float32)
    output = jnp.sum(gate_vals.astype(jnp.float32)[:, :, None] * slot_out, axis=1).astype(
        jnp.bfloat16
    )
    grad_gates = jnp.sum(cotangent.astype(jnp.float32)[:, None, :] * slot_out, axis=2)
    gate_rows = gate_pad[source].astype(jnp.float32)
    send_grad = (gate_rows[:, None] * cot_pad[token_of].astype(jnp.float32)).astype(jnp.bfloat16)
    grad_in = lax.all_to_all(
        send_grad.reshape(groups, WAVE * MOST, model_width),
        "expert",
        split_axis=0,
        concat_axis=0,
        tiled=True,
    )
    out_grad = grad_in.reshape(groups, WAVE, MOST, model_width)
    hidden_grad = jnp.einsum(
        "skmd,kdf->skmf", out_grad, full_down, preferred_element_type=jnp.float32
    )
    gate_grad = (hidden_grad * up_pre * sigmoid_g * (1.0 + gate_pre * (1.0 - sigmoid_g))).astype(
        jnp.bfloat16
    )
    up_grad = (hidden_grad * gate_pre * sigmoid_g).astype(jnp.bfloat16)
    row_grad = (
        jnp.einsum("skmf,kdf->skmd", gate_grad, full_gate, preferred_element_type=jnp.float32)
        + jnp.einsum("skmf,kdf->skmd", up_grad, full_up, preferred_element_type=jnp.float32)
    ).astype(jnp.bfloat16)
    grads_home = lax.all_to_all(
        row_grad.reshape(groups, WAVE * MOST, model_width),
        "expert",
        split_axis=0,
        concat_axis=0,
        tiled=True,
    )
    grads_pad = jnp.concatenate([grads_home.reshape(-1, model_width), zero_row], axis=0)
    grad_tokens = jnp.sum(
        grads_pad[target].reshape(tok_count, TOP, model_width).astype(jnp.float32), axis=1
    ).astype(jnp.bfloat16)
    term_gate = jnp.einsum("skmd,skmf->kdf", rows_in, gate_grad, preferred_element_type=jnp.float32)
    term_up = jnp.einsum("skmd,skmf->kdf", rows_in, up_grad, preferred_element_type=jnp.float32)
    term_down = jnp.einsum("skmd,skmf->kdf", out_grad, hidden, preferred_element_type=jnp.float32)
    grad_w_gate, grad_w_up, grad_w_down = (
        lax.psum_scatter(
            term_gate.astype(jnp.bfloat16), "fsdp", scatter_dimension=1, tiled=True
        ).astype(jnp.float32),
        lax.psum_scatter(
            term_up.astype(jnp.bfloat16), "fsdp", scatter_dimension=1, tiled=True
        ).astype(jnp.float32),
        lax.psum_scatter(
            term_down.astype(jnp.bfloat16), "fsdp", scatter_dimension=1, tiled=True
        ).astype(jnp.float32),
    )
    return (output, grad_tokens, grad_gates, grad_w_gate, grad_w_up, grad_w_down)


def solution(mesh):
    placed = (
        P(("expert", "fsdp"), None),
        P(("expert", "fsdp"), None),
        P(("expert", "fsdp"), None),
        P("expert", "fsdp", None),
        P("expert", "fsdp", None),
        P("expert", "fsdp", None),
        P(("expert", "fsdp"), None),
    )
    return jax.shard_map(
        on_device,
        mesh=mesh,
        in_specs=placed,
        out_specs=(
            P(("expert", "fsdp"), None),
            P(("expert", "fsdp"), None),
            P(("expert", "fsdp"), None),
            P("expert", "fsdp", None),
            P("expert", "fsdp", None),
            P("expert", "fsdp", None),
        ),
        check_vma=False,
    )
```

profile of v0, /device:TPU:0, one launch (start us, length us, event | category | flops | bytes accessed | tf_op | source)
XLA Modules:
  0.0 348.4 jit_solution(2451086021296024505)
XLA Ops:
  7.2 0.0 all-gather.8.cloned.1.call-start
  7.2 0.7 all-gather.8.cloned.1.call-update
  7.9 0.0 all-gather.6.cloned.1.call-start
  7.9 0.7 all-gather.6.cloned.1.call-update
  8.6 0.0 all-gather.4.cloned.1.call-start
  8.7 0.7 all-gather.4.cloned.1.call-update
  9.4 0.8 copy.20
  10.2 0.1 reshape.313
  10.4 0.1 reshape.312
  10.5 0.1 reshape.311
  10.7 1.2 reduce-window.6
  11.8 0.2 slice_reduce_fusion
  12.0 0.2 reduce-window.9
  12.2 0.8 copy.23
  13.1 0.2 reshape.321
  13.2 0.1 add_bitcast_fusion
  13.4 0.1 fusion.52
  13.5 6.2 %scatter_custom_fusion = s32[192]{0:T(256)S(1)} fusion(s32[1536]{0:T(1024)S(1)} %get-tuple-element.15, s32[1536]{0:T(1024)S(1)} %iota.11, s32[]{:T(128)} %constant.32.clone.1), kind=kCustom, calls=%fused_computation.92 | custom fusion | bytes 772 | tf_op jit(solution)/shard_map/scatter | solution.py:27
  19.7 1.6 gather_fusion.2
  21.3 0.1 reshape.327
  21.4 1.4 concatenate.18
  22.8 1.1 gather_fusion.3
  23.9 1.1 fusion.33
  25.0 6.3 %all-to-all-start.2 = ((bf16[4,48,2048]{2,1,0:T(8,128)(2,1)}), bf16[4,48,2048]{2,1,0:T(8,128)(2,1)S(1)}, u32[]{:S(2)}, u32[]{:S(2)}) async-start(bf16[4,48,2048]{2,1,0:T(8,128)(2,1)} %fusion.33), calls=%async_computation.2 | async-start | bytes 1572864 | tf_op jit(solution)/shard_map/all_to_all | solution.py:71
  31.4 0.1 concatenate.15
  31.5 2.0 gather_fusion
  33.5 18.0 %all-to-all-done.2 = bf16[4,48,2048]{2,1,0:T(8,128)(2,1)S(1)} async-done(((bf16[4,48,2048]{2,1,0:T(8,128)(2,1)}), bf16[4,48,2048]{2,1,0:T(8,128)(2,1)S(1)}, u32[]{:S(2)}, u32[]{:S(2)}) %all-to-all-start.2) | async-done | bytes 786464 | tf_op jit(solution)/shard_map/all_to_all | solution.py:71
  51.5 3.5 %all-to-all-start = ((bf16[4,48,2048]{2,1,0:T(8,128)(2,1)}), bf16[4,48,2048]{2,1,0:T(8,128)(2,1)S(1)}, u32[]{:S(2)}, u32[]{:S(2)}) async-start(bf16[4,48,2048]{2,1,0:T(8,128)(2,1)} %bitcast.1), calls=%async_computation | async-start | bytes 1572864 | tf_op jit(solution)/shard_map/all_to_all | solution.py:42
  55.0 0.0 reduce-scatter.4.cloned.1.call-start
  55.0 0.8 all-gather.8.cloned.1.call-done
  55.8 5.0 %fusion.21 = f32[4,1,48,1408]{3,2,0,1:T(8,128)} fusion(bf16[4,48,2048]{2,1,0:T(8,128)(2,1)S(1)} %all-to-all-done.2, bf16[1,2048,1408]{2,1,0:T(8,128)(2,1)} %all-gather.8.cloned.1.call-done), kind=kOutput, calls=%fused_computation.28 | convolution fusion | flops 1107296256 | bytes 7634944 | tf_op jit(solution)/shard_map/skmd,kdf->skmf/dot_general | solution.py:79
  60.8 13.8 %all-to-all-done = bf16[4,48,2048]{2,1,0:T(8,128)(2,1)S(1)} async-done(((bf16[4,48,2048]{2,1,0:T(8,128)(2,1)}), bf16[4,48,2048]{2,1,0:T(8,128)(2,1)S(1)}, u32[]{:S(2)}, u32[]{:S(2)}) %all-to-all-start) | async-done | bytes 786464 | tf_op jit(solution)/shard_map/all_to_all | solution.py:42
  74.6 26.3 %all-gather.6.cloned.1.call-done = bf16[1,2048,1408]{2,1,0:T(8,128)(2,1)} async-done(((bf16[1,256,1408]{2,1,0:T(8,128)(2,1)}), bf16[1,2048,1408]{2,1,0:T(8,128)(2,1)}) %all-gather.6.cloned.1.call-update) | async-done | bytes 5767184 | tf_op jit(solution)/shard_map/all_gather | solution.py:46
  100.9 5.0 %fusion.18 = f32[4,1,48,1408]{3,2,0,1:T(8,128)} fusion(bf16[4,48,2048]{2,1,0:T(8,128)(2,1)S(1)} %all-to-all-done, bf16[1,2048,1408]{2,1,0:T(8,128)(2,1)} %all-gather.6.cloned.1.call-done), kind=kOutput, calls=%fused_computation.27 | convolution fusion | flops 1107296256 | bytes 7634944 | tf_op jit(solution)/shard_map/skmd,kdf->skmf/dot_general | solution.py:50
  105.9 40.1 %all-gather.4.cloned.1.call-done = bf16[1,2048,1408]{2,1,0:T(8,128)(2,1)} async-done(((bf16[1,256,1408]{2,1,0:T(8,128)(2,1)}), bf16[1,2048,1408]{2,1,0:T(8,128)(2,1)}) %all-gather.4.cloned.1.call-update) | async-done | bytes 5767184 | tf_op jit(solution)/shard_map/all_gather | solution.py:45
  146.0 5.0 %multiply_convert_fusion.1 = (bf16[4,1,48,1408]{3,2,0,1:T(8,128)(2,1)S(1)}, bf16[4,1,48,1408]{3,2,0,1:T(8,128)(2,1)S(1)}, bf16[4,1,48,1408]{3,2,0,1:T(8,128)(2,1)S(1)}) fusion(f32[4,1,48,1408]{3,2,0,1:T(8,128)} %fusion.21, f32[4,1,48,1408]{3,2,0,1:T(8,128)} %fusion.18, bf16[4,48,2048]{2,1,0:T(8,128)(2,1)S(1)} %all-to-all-done, ...), kind=kOutput, calls=%fused_computation.35 | convolution fusion | flops 1111621632 | bytes 10338304 | tf_op jit(solution)/shard_map/skmd,kdf->skmf/dot_general | solution.py:49
  151.0 4.4 %fusion = bf16[1,2048,1408]{2,1,0:T(8,128)(2,1)} fusion(bf16[4,48,2048]{2,1,0:T(8,128)(2,1)S(1)} %all-to-all-done, bf16[4,1,48,1408]{3,2,0,1:T(8,128)(2,1)S(1)} %get-tuple-element.16), kind=kOutput, calls=%fused_computation.11 | convolution fusion | flops 1110179840 | bytes 7094272 | tf_op jit(solution)/shard_map/skmd,skmf->kdf/dot_general | solution.py:101
  155.4 0.0 reduce-scatter.6.cloned.1.call-start
  155.5 4.3 %fusion.1 = bf16[1,2048,1408]{2,1,0:T(8,128)(2,1)} fusion(bf16[4,48,2048]{2,1,0:T(8,128)(2,1)S(1)} %all-to-all-done, bf16[4,1,48,1408]{3,2,0,1:T(8,128)(2,1)S(1)} %get-tuple-element.18), kind=kOutput, calls=%fused_computation.12 | convolution fusion | flops 1110179840 | bytes 7094272 | tf_op jit(solution)/shard_map/skmd,skmf->kdf/dot_general | solution.py:102
  159.8 0.2 reduce-scatter.8.cloned.1.call-start
  160.0 0.9 copy-done.3
  160.9 4.7 %fusion.2 = bf16[1,2048,1408]{2,1,0:T(8,128)(2,1)} fusion(bf16[4,48,2048]{2,1,0:T(8,128)(2,1)S(1)} %copy-done.3, bf16[4,1,48,1408]{3,2,0,1:T(8,128)(2,1)S(1)} %get-tuple-element.17), kind=kOutput, calls=%fused_computation.13 | convolution fusion | flops 1110179840 | bytes 7094272 | tf_op jit(solution)/shard_map/skmd,skmf->kdf/dot_general | solution.py:103
  165.6 5.6 %fusion.7 = f32[4,48,2048]{2,1,0:T(8,128)S(1)} fusion(bf16[1,2048,1408]{2,1,0:T(8,128)(2,1)} %all-gather.6.cloned.1.call-done, bf16[4,1,48,1408]{3,2,0,1:T(8,128)(2,1)S(1)} %get-tuple-element.18), kind=kOutput, calls=%fused_computation.18 | convolution fusion | flops 1107296256 | bytes 7880704 | tf_op jit(solution)/shard_map/skmf,kdf->skmd/dot_general | solution.py:88
  171.3 2.9 fusion.27
  174.2 4.6 %all-to-all-start.3 = ((bf16[4,48,2048]{2,1,0:T(8,128)(2,1)}), bf16[4,48,2048]{2,1,0:T(8,128)(2,1)S(1)}, u32[]{:S(2)}, u32[]{:S(2)}) async-start(bf16[4,48,2048]{2,1,0:T(8,128)(2,1)} %fusion.27), calls=%async_computation.3 | async-start | bytes 1572864 | tf_op jit(solution)/shard_map/all_to_all | solution.py:90
  178.8 5.9 %fusion.30 = bf16[4,48,2048]{2,1,0:T(8,128)(2,1)} fusion(bf16[1,2048,1408]{2,1,0:T(8,128)(2,1)} %all-gather.8.cloned.1.call-done, bf16[4,1,48,1408]{3,2,0,1:T(8,128)(2,1)S(1)} %copy-done.6), kind=kOutput, calls=%fused_computation.31 | convolution fusion | flops 1107689472 | bytes 7094272 | tf_op jit(solution)/shard_map/skmf,kdf->skmd/dot_general | solution.py:53
  184.8 14.6 %all-to-all-done.3 = bf16[4,48,2048]{2,1,0:T(8,128)(2,1)S(1)} async-done(((bf16[4,48,2048]{2,1,0:T(8,128)(2,1)}), bf16[4,48,2048]{2,1,0:T(8,128)(2,1)S(1)}, u32[]{:S(2)}, u32[]{:S(2)}) %all-to-all-start.3) | async-done | bytes 786464 | tf_op jit(solution)/shard_map/all_to_all | solution.py:90
  199.4 4.2 %all-to-all-start.1 = ((bf16[4,48,2048]{2,1,0:T(8,128)(2,1)}), bf16[4,48,2048]{2,1,0:T(8,128)(2,1)}, u32[]{:S(2)}, u32[]{:S(2)}) async-start(bf16[4,48,2048]{2,1,0:T(8,128)(2,1)} %fusion.30), calls=%async_computation.1 | async-start | bytes 1572864 | tf_op jit(solution)/shard_map/all_to_all | solution.py:56
  203.6 1.5 convert_element_type.110
  205.1 0.1 copy.19
  205.2 1.2 concatenate.19
  206.4 7.0 %gather_fusion.4 = bf16[1536,2048]{1,0:T(8,128)(2,1)} fusion(bf16[193,2048]{1,0:T(8,128)(2,1)S(1)} %concatenate.19, s32[2048]{0:T(1024)S(1)} %pad_clamp_fusion), kind=kCustom, calls=%fused_computation.4 | custom fusion | bytes 12589056 | tf_op jit(solution)/shard_map/gather | solution.py:99
  213.5 11.0 %reshape.325 = bf16[256,6,2048]{2,1,0:T(8,128)(2,1)} reshape(bf16[1536,2048]{1,0:T(8,128)(2,1)} %gather_fusion.4) | data formatting | bytes 12582912 | tf_op jit(solution)/shard_map/reshape | solution.py:99
  224.5 10.9 %reduce_sum.44 = bf16[256,2048]{1,0:T(8,128)(2,1)} reduce(bf16[256,6,2048]{2,1,0:T(8,128)(2,1)} %reshape.325, bf16[]{:T(256)} %constant.31.clone.1), dimensions={1}, to_apply=%region_5.6 | reduce | flops 2621440 | bytes 7340034 | tf_op jit(solution)/shard_map/reduce_sum | solution.py:98
  235.4 1.2 concatenate.16
  236.6 7.1 %gather_fusion.1 = bf16[1536,2048]{1,0:T(8,128)(2,1)} fusion(bf16[193,2048]{1,0:T(8,128)(2,1)S(1)} %concatenate.16, s32[2048]{0:T(1024)S(1)} %pad_clamp_fusion), kind=kCustom, calls=%fused_computation.1 | custom fusion | bytes 12589056 | tf_op jit(solution)/shard_map/gather | solution.py:64
  243.6 11.7 %reshape.326 = f32[256,6,2048]{2,1,0:T(8,128)} reshape(bf16[1536,2048]{1,0:T(8,128)(2,1)} %gather_fusion.1) | data formatting | bytes 18874368 | tf_op jit(solution)/shard_map/convert_element_type | solution.py:64
  255.4 11.8 %multiply_reduce_fusion = (f32[256,6]{1,0:T(8,128)S(1)}, bf16[256,2048]{1,0:T(8,128)(2,1)}) fusion(f32[256,6,2048]{2,1,0:T(8,128)} %reshape.326, f32[256,2048]{1,0:T(8,128)S(1)} %convert_element_type.110, f32[256,6]{1,0:T(8,128)S(1)} %copy.19), kind=kLoop, calls=%fused_computation.6 | loop fusion | flops 12057088 | bytes 15740928 | tf_op jit(solution)/shard_map/reduce_sum | solution.py:68
  267.2 0.7 copy.24
  267.9 2.3 convert_element_type.113
  270.2 6.7 %reduce-scatter.6.cloned.1.call-done = bf16[1,256,1408]{2,1,0:T(8,128)(2,1)} async-done(((bf16[1,2048,1408]{2,1,0:T(8,128)(2,1)}), bf16[1,256,1408]{2,1,0:T(8,128)(2,1)}) %reduce-scatter.6.cloned.1.call-update) | async-done | bytes 720912 | tf_op jit(solution)/shard_map/reduce_scatter | solution.py:108
  276.9 2.3 convert_element_type.116
  279.2 60.1 %reduce-scatter.8.cloned.1.call-done = bf16[1,256,1408]{2,1,0:T(8,128)(2,1)} async-done(((bf16[1,2048,1408]{2,1,0:T(8,128)(2,1)}), bf16[1,256,1408]{2,1,0:T(8,128)(2,1)}) %reduce-scatter.8.cloned.1.call-update) | async-done | bytes 720912 | tf_op jit(solution)/shard_map/reduce_scatter | solution.py:111
  339.3 2.3 convert_element_type.119
  (32 shorter events, 0.2 us)
Async XLA Ops:
  7.2 48.6 %all-gather.8.cloned.1.call-start = ((), (), s32[]{:S(2)}) async-start(), calls=%async_computation.9 | async-start | bytes 6488064 | tf_op jit(solution)/shard_map/all_gather | solution.py:47
  7.9 93.0 %all-gather.6.cloned.1.call-start = ((), (), s32[]{:S(2)}) async-start(), calls=%async_computation.8 | async-start | bytes 6488064 | tf_op jit(solution)/shard_map/all_gather | solution.py:46
  8.6 137.4 %all-gather.4.cloned.1.call-start = ((), (), s32[]{:S(2)}) async-start(), calls=%async_computation.7 | async-start | bytes 6488064 | tf_op jit(solution)/shard_map/all_gather | solution.py:45
  21.4 10.0 %copy-start.1 = (bf16[256,2048]{1,0:T(8,128)(2,1)S(1)}, bf16[256,2048]{1,0:T(8,128)(2,1)}, u32[]{:S(2)}) copy-start(bf16[256,2048]{1,0:T(8,128)(2,1)} %param.7) | copy-start | bytes 3145732
  25.0 26.5 %all-to-all-start.2 = ((bf16[4,48,2048]{2,1,0:T(8,128)(2,1)}), bf16[4,48,2048]{2,1,0:T(8,128)(2,1)S(1)}, u32[]{:S(2)}, u32[]{:S(2)}) async-start(bf16[4,48,2048]{2,1,0:T(8,128)(2,1)} %fusion.33), calls=%async_computation.2 | async-start | bytes 1572864 | tf_op jit(solution)/shard_map/all_to_all | solution.py:71
  51.5 54.5 %copy-start.2 = (bf16[4,48,2048]{2,1,0:T(8,128)(2,1)}, bf16[4,48,2048]{2,1,0:T(8,128)(2,1)S(1)}, u32[]{:S(2)}) copy-start(bf16[4,48,2048]{2,1,0:T(8,128)(2,1)S(1)} %all-to-all-done.2) | copy-start | bytes 2359300
  51.5 23.1 %all-to-all-start = ((bf16[4,48,2048]{2,1,0:T(8,128)(2,1)}), bf16[4,48,2048]{2,1,0:T(8,128)(2,1)S(1)}, u32[]{:S(2)}, u32[]{:S(2)}) async-start(bf16[4,48,2048]{2,1,0:T(8,128)(2,1)} %bitcast.1), calls=%async_computation | async-start | bytes 1572864 | tf_op jit(solution)/shard_map/all_to_all | solution.py:42
  55.0 212.9 %reduce-scatter.4.cloned.1.call-start = ((), (), s32[]{:S(2)}) async-start(), calls=%async_computation.10 | async-start | bytes 6488064 | tf_op jit(solution)/shard_map/reduce_scatter | solution.py:105
  151.0 9.0 %copy-start.5 = (bf16[4,1,48,1408]{3,2,0,1:T(8,128)(2,1)}, bf16[4,1,48,1408]{3,2,0,1:T(8,128)(2,1)S(1)}, u32[]{:S(2)}) copy-start(bf16[4,1,48,1408]{3,2,0,1:T(8,128)(2,1)S(1)} %get-tuple-element.17) | copy-start | bytes 1622020
  155.4 121.5 %reduce-scatter.6.cloned.1.call-start = ((), (), s32[]{:S(2)}) async-start(), calls=%async_computation.11 | async-start | bytes 6488064 | tf_op jit(solution)/shard_map/reduce_scatter | solution.py:108
  159.8 1.2 copy-start.3
  159.8 179.5 %reduce-scatter.8.cloned.1.call-start = ((), (), s32[]{:S(2)}) async-start(), calls=%async_computation.12 | async-start | bytes 6488064 | tf_op jit(solution)/shard_map/reduce_scatter | solution.py:111
  165.6 5.6 %slice-start = ((s8[5767168]{0:T(1024)(128)(4,1)}), s8[1572864]{0:T(1024)(128)(4,1)S(1)}, s32[]{:S(2)}) async-start(s8[5767168]{0:T(1024)(128)(4,1)} %bitcast.109), calls=%async_computation.13 | async-start | bytes 3145728
  165.6 5.6 %slice-start.1 = ((s8[5767168]{0:T(1024)(128)(4,1)}), s8[4194304]{0:T(1024)(128)(4,1)S(1)}, s32[]{:S(2)}) async-start(s8[5767168]{0:T(1024)(128)(4,1)} %bitcast.109), calls=%async_computation.14 | async-start | bytes 8388608
  171.2 7.6 %copy-start.6 = (bf16[4,1,48,1408]{3,2,0,1:T(8,128)(2,1)S(1)}, bf16[4,1,48,1408]{3,2,0,1:T(8,128)(2,1)}, u32[]{:S(2)}) copy-start(bf16[4,1,48,1408]{3,2,0,1:T(8,128)(2,1)} %copy-done.5) | copy-start | bytes 1622020
  174.2 25.2 %all-to-all-start.3 = ((bf16[4,48,2048]{2,1,0:T(8,128)(2,1)}), bf16[4,48,2048]{2,1,0:T(8,128)(2,1)S(1)}, u32[]{:S(2)}, u32[]{:S(2)}) async-start(bf16[4,48,2048]{2,1,0:T(8,128)(2,1)} %fusion.27), calls=%async_computation.3 | async-start | bytes 1572864 | tf_op jit(solution)/shard_map/all_to_all | solution.py:90
  178.8 26.2 %copy-start.4 = (bf16[256,6]{0,1:T(8,128)(2,1)S(1)}, bf16[256,6]{0,1:T(8,128)(2,1)}, u32[]{:S(2)}) copy-start(bf16[256,6]{0,1:T(8,128)(2,1)} %param.9) | copy-start | bytes 9220
  199.4 5.8 %copy-start = (bf16[4,48,2048]{2,1,0:T(8,128)(2,1)}, bf16[4,48,2048]{2,1,0:T(8,128)(2,1)S(1)}, u32[]{:S(2)}) copy-start(bf16[4,48,2048]{2,1,0:T(8,128)(2,1)S(1)} %all-to-all-done.3) | copy-start | bytes 2359300
  199.4 36.0 %all-to-all-start.1 = ((bf16[4,48,2048]{2,1,0:T(8,128)(2,1)}), bf16[4,48,2048]{2,1,0:T(8,128)(2,1)}, u32[]{:S(2)}, u32[]{:S(2)}) async-start(bf16[4,48,2048]{2,1,0:T(8,128)(2,1)} %fusion.30), calls=%async_computation.1 | async-start | bytes 1572864 | tf_op jit(solution)/shard_map/all_to_all | solution.py:56
Sparse Core Ops, SparseCore 0:
  9.9 45.9 all-gather.7
  57.7 43.1 all-gather.5
  102.8 43.1 all-gather.3
  155.5 58.9 reduce-scatter.3
  217.8 59.0 reduce-scatter.5
  280.2 59.0 reduce-scatter.7
where the time goes:
time: 350 us; the launch traced here: 348 us
  waiting for transfers between devices  182 us (52%)
  local copies, waits for them, and re-layouts  55.9 us (16%)
  matrix products  42.8 us (12%)
  other arithmetic  33.8 us (10%)
  starting transfers between devices  19.1 us (5%)
  between operations  14.4 us (4%)
    reduce_scatter x1, waiting for transfers between devices, on_device(): lax.psum_scatter(term_down.astype(jnp.bfloat16), 'fsdp', scatter_dimensio...  60.1 us
    all_gather x1, waiting for transfers between devices, on_device(): lax.all_gather(w_gate, 'fsdp', axis=1, tiled=True)  40.1 us
    all_gather x1, waiting for transfers between devices, on_device(): lax.all_gather(w_up, 'fsdp', axis=1, tiled=True)  26.3 us
    all_to_all x1, waiting for transfers between devices, on_device(): lax.all_to_all(send_grad.reshape(groups, WAVE * MOST, model_width), 'expe...  18 us
    all_to_all x1, waiting for transfers between devices, on_device(): lax.all_to_all(row_grad.reshape(groups, WAVE * MOST, model_width), 'exper...  14.6 us
    all_to_all x1, waiting for transfers between devices, on_device(): lax.all_to_all(send_rows, 'expert', split_axis=0, concat_axis=0, tiled=True)  13.8 us
    reduce_sum x1, other arithmetic, on_device(): jnp.sum(cotangent.astype(jnp.float32)[:, None, :] * slot_out, axis=2)  11.8 us
    convert_element_type x1, local copies, waits for them, and re-layouts, on_device(): back_pad[target].reshape(tok_count, TOP, model_width).astype(jnp.float32)  11.7 us
  transfers between devices with their start and end apart: 10, of which 8 were waited for; matrix products, arithmetic and copies ran while one was open for 34% of the time, Pallas kernels for 0%

commit v1 on v0

v1 whole, which is shorter than its diff:
```python
import jax
import jax.numpy as jnp
from jax import lax
from jax.sharding import PartitionSpec as P

EXPERTS = 64
WAVE = 1
MOST = 48
F32 = jnp.float32
BF16 = jnp.bfloat16


def dot(a, b, dims):
    return lax.dot_general(a, b, (dims, ((), ())), preferred_element_type=F32)


def routes(expert_ids, gate_vals, groups):
    per_index = EXPERTS // groups
    window = WAVE * groups
    tok_count = expert_ids.shape[0]
    local_index = expert_ids % per_index
    window_slot = jnp.where(
        local_index < WAVE, expert_ids // per_index * WAVE + local_index, window
    )
    slot_is = window_slot[:, :, None] == jnp.arange(window, dtype=jnp.int32)[None, None, :]
    chosen = jnp.any(slot_is, axis=1)
    gate_of = jnp.sum(jnp.where(slot_is, gate_vals.astype(F32)[:, :, None], 0.0), axis=1)
    tok = jnp.arange(tok_count, dtype=jnp.int32)
    before = (tok[:, None] > tok[None, :]).astype(BF16)
    rank = dot(before, chosen.astype(BF16), ((1,), (0,))).astype(jnp.int32)
    place = chosen[:, :, None] & (
        rank[:, :, None] == jnp.arange(MOST, dtype=jnp.int32)[None, None, :]
    )
    pick = place.astype(BF16).reshape(tok_count, window * MOST)
    weighted = (
        jnp.where(place, gate_of[:, :, None], 0.0).astype(BF16).reshape(tok_count, window * MOST)
    )
    return slot_is, place, pick, weighted


def on_device(tokens, expert_ids, gate_vals, w_gate, w_up, w_down, cotangent):
    groups = lax.axis_size("expert")
    columns = lax.axis_size("fsdp")
    side = lax.axis_index("fsdp") % 2
    tok_count, width = tokens.shape
    block = w_gate.shape[1]
    rows = groups * MOST
    sides = [[i for i in range(columns) if i % 2 == s] for s in (0, 1)]
    pairs = [(i, i ^ 1) for i in range(columns)]

    def swap(x):
        return lax.ppermute(x, "fsdp", pairs)

    def gather(w):
        return lax.all_gather(w[0], "fsdp", axis_index_groups=sides, axis=0, tiled=True)

    def scatter(x):
        return lax.psum_scatter(
            x.astype(BF16), "fsdp", scatter_dimension=0, axis_index_groups=sides, tiled=True
        ).astype(F32)[None]

    def halves(x):
        cut = x.reshape(x.shape[0], columns // 2, 2, block)
        even = cut[:, :, 0].reshape(x.shape[0], width // 2)
        odd = cut[:, :, 1].reshape(x.shape[0], width // 2)
        return jnp.where(side == 0, even, odd), jnp.where(side == 0, odd, even)

    def whole_rows(mine, other):
        even = jnp.where(side == 0, mine, other).reshape(-1, columns // 2, 1, block)
        odd = jnp.where(side == 0, other, mine).reshape(-1, columns // 2, 1, block)
        return jnp.concatenate([even, odd], axis=2).reshape(-1, width)

    def exchange(mine, other):
        packed = jnp.stack(
            [mine.reshape(groups, MOST, width // 2), other.reshape(groups, MOST, width // 2)],
            axis=1,
        )
        there = lax.all_to_all(packed, "expert", split_axis=0, concat_axis=0, tiled=True)
        return there[:, 0].reshape(rows, width // 2), there[:, 1].reshape(rows, width // 2)

    full_gate, full_up, full_down = gather(w_gate), gather(w_up), gather(w_down)
    slot_is, place, pick, weighted = routes(expert_ids, gate_vals, groups)
    tok_mine, tok_other = halves(tokens)
    cot_mine, cot_other = halves(cotangent)
    first = ((0,), (0,))
    row_mine, row_other = exchange(
        dot(pick, tok_mine, first).astype(BF16), dot(pick, tok_other, first).astype(BF16)
    )
    og_mine, og_other = exchange(
        dot(weighted, cot_mine, first).astype(BF16), dot(weighted, cot_other, first).astype(BF16)
    )
    row_in = jnp.concatenate([row_mine, swap(row_other)], axis=0)
    out_grad = jnp.concatenate([og_mine, swap(og_other)], axis=0)

    def summed(x):
        return x[:rows] + swap(x[rows:].astype(BF16)).astype(F32)

    def both(x):
        return jnp.concatenate([x, swap(x)], axis=0)

    plain, turned = ((1,), (0,)), ((1,), (1,))
    gate_pre = summed(dot(row_in, full_gate, plain))
    up_pre = summed(dot(row_in, full_up, plain))
    sigmoid_g = jax.nn.sigmoid(gate_pre)
    hidden = both((gate_pre * sigmoid_g * up_pre).astype(BF16))
    grad_w_down = scatter(dot(out_grad, hidden, first))
    hidden_grad = summed(dot(out_grad, full_down, plain))
    gate_grad = both(
        (hidden_grad * up_pre * sigmoid_g * (1.0 + gate_pre * (1.0 - sigmoid_g))).astype(BF16)
    )
    grad_w_gate = scatter(dot(row_in, gate_grad, first))
    up_grad = both((hidden_grad * gate_pre * sigmoid_g).astype(BF16))
    grad_w_up = scatter(dot(row_in, up_grad, first))

    expert_out = dot(hidden, full_down, turned).astype(BF16)
    out_mine, out_other = exchange(expert_out[:rows], swap(expert_out[rows:]))
    slot_grad = (dot(gate_grad, full_gate, turned) + dot(up_grad, full_up, turned)).astype(BF16)
    sg_mine, sg_other = exchange(slot_grad[:rows], swap(slot_grad[rows:]))

    output = whole_rows(
        dot(weighted, out_mine, plain).astype(BF16), dot(weighted, out_other, plain).astype(BF16)
    )
    grad_tokens = whole_rows(
        dot(pick, sg_mine, plain).astype(BF16), dot(pick, sg_other, plain).astype(BF16)
    )
    met = dot(cot_mine, out_mine, turned) + dot(cot_other, out_other, turned)
    met = jnp.sum(jnp.where(place, met.reshape(place.shape), 0.0), axis=2)
    grad_gates = jnp.sum(jnp.where(slot_is, met[:, None, :], 0.0), axis=2)
    return (output, grad_tokens, grad_gates, grad_w_gate, grad_w_up, grad_w_down)


def solution(mesh):
    token = P(("expert", "fsdp"), None)
    weight = P("expert", "fsdp", None)
    return jax.shard_map(
        on_device,
        mesh=mesh,
        in_specs=(token, token, token, weight, weight, weight, token),
        out_specs=(token, token, token, weight, weight, weight),
        check_vma=False,
    )
```

time: 350 us -> 343 us (0.980)
  blocking collectives: 0 us -> 48.5 us
  local copies, waits for them, and re-layouts: 55.9 us -> 15.6 us
  waiting for transfers between devices: 182 us -> 205 us
  other arithmetic: 33.8 us -> 16.4 us
  matrix products: 42.8 us -> 33.1 us
  starting transfers between devices: 19.1 us -> 9.76 us
    all_to_all x0 -> x2, blocking collectives: none -> 48.5 us  [exchange(): lax.all_to_all(packed, 'expert', split_axis=0, concat_axis=0, tiled=True)]
    reduce_sum x3 -> x2, other arithmetic: 22.7 us -> 0.69 us  [the longest x1 0.63 us: on_device(): grad_gates = jnp.sum(jnp.where(slot_is, met[:, None, :], 0.0), axis=2)]
    all_gather x3, waiting for transfers between devices: 67.2 us -> 87.4 us  [gather(): lax.all_gather(w[0], 'fsdp', axis_index_groups=sides, axis=0, tiled=True)]
    gather x5 -> x0, local copies, waits for them, and re-layouts: 18.9 us -> none  [the longest x1 7.06 us: on_device(): back_pad[target].reshape(tok_count, TOP, model_width).astype(jnp.float32)]
    ppermute x0 -> x10, waiting for transfers between devices: none -> 14 us  [swap(): return lax.ppermute(x, 'fsdp', pairs)]
    convert_element_type x3 -> x0, local copies, waits for them, and re-layouts: 11.9 us -> none  [the longest x1 11.7 us: on_device(): back_pad[target].reshape(tok_count, TOP, model_width).astype(jnp.float32)]
    all_to_all x4 -> x2, waiting for transfers between devices: 46.4 us -> 35.5 us  [exchange(): lax.all_to_all(packed, 'expert', split_axis=0, concat_axis=0, tiled=True)]
    all_to_all x4 -> x2, starting transfers between devices: 18.7 us -> 8.31 us  [exchange(): lax.all_to_all(packed, 'expert', split_axis=0, concat_axis=0, tiled=True)]
  transfers between devices with their start and end apart: 10 -> 18, of which waited for: 8 -> 15; matrix products, arithmetic and copies ran while one was open for 34% -> 14% of each run, Pallas kernels for 0% -> 0%
where the time goes in v1:
time: 343 us
  waiting for transfers between devices  205 us (60%)
  blocking collectives  48.5 us (14%)
  matrix products  33.1 us (10%)
  other arithmetic  16.4 us (5%)
  local copies, waits for them, and re-layouts  15.6 us (5%)
  between operations  14.6 us (4%)
  starting transfers between devices  9.76 us (3%)
    all_gather x3, waiting for transfers between devices, gather(): lax.all_gather(w[0], 'fsdp', axis_index_groups=sides, axis=0, tiled=True)  87.4 us
    reduce_scatter x3, waiting for transfers between devices, scatter(): lax.psum_scatter(x.astype(BF16), 'fsdp', scatter_dimension=0, axis_index_...  65.6 us
    all_to_all x2, blocking collectives, exchange(): lax.all_to_all(packed, 'expert', split_axis=0, concat_axis=0, tiled=True)  48.5 us
    all_to_all x2, waiting for transfers between devices, exchange(): lax.all_to_all(packed, 'expert', split_axis=0, concat_axis=0, tiled=True)  35.5 us
    dot_general x20, matrix products, dot(): return lax.dot_general(a, b, (dims, ((), ())), preferred_element_type=F32)  33.1 us
    ppermute x10, waiting for transfers between devices, swap(): return lax.ppermute(x, 'fsdp', pairs)  14 us
    all_to_all x2, starting transfers between devices, exchange(): lax.all_to_all(packed, 'expert', split_axis=0, concat_axis=0, tiled=True)  8.31 us
    broadcast_in_dim x3, other arithmetic, scatter(): lax.psum_scatter(x.astype(BF16), 'fsdp', scatter_dimension=0, axis_index_...  6.91 us
  transfers between devices with their start and end apart: 18, of which 15 were waited for; matrix products, arithmetic and copies ran while one was open for 14% of the time, Pallas kernels for 0%

profile of v1, /device:TPU:0, one launch (start us, length us, event | category | flops | bytes accessed | tf_op | source)
XLA Modules:
  0.0 342.5 jit_solution(18091115151017018275)
XLA Ops:
  7.2 0.7 all-gather.9.cloned.1.call-update
  8.0 0.7 all-gather.7.cloned.1.call-update
  8.7 0.7 all-gather.11.cloned.1.call-update
  9.7 0.5 copy.42
  10.2 1.5 copy.48
  11.9 0.3 convolution_convert_fusion.9
  12.2 0.3 convolution_convert_fusion.10
  12.6 26.3 %all_to_all.20 = bf16[4,2,48,1024]{3,2,1,0:T(8,128)(2,1)S(1)} all-to-all(bf16[4,2,48,1024]{3,2,1,0:T(8,128)(2,1)S(1)} %pad_maximum_fusion.5), channel_id=1, replica_groups=mesh['expert'=4,'fsdp'=8] {'expert'}, dimensions={0} | all-to-all | bytes 1572864 | tf_op jit(solution)/shard_map/all_to_all | solution.py:78
  38.9 0.8 fusion.35
  39.7 1.7 collective-permute-done
  41.4 12.8 %all-gather.9.cloned.1.call-done = bf16[1,1024,1408]{2,1,0:T(8,128)(2,1)} async-done(((bf16[1,256,1408]{2,1,0:T(8,128)(2,1)}), bf16[1,1024,1408]{2,1,0:T(8,128)(2,1)}) %all-gather.9.cloned.1.call-update) | async-done | bytes 2883600 | tf_op jit(solution)/shard_map/all_gather | solution.py:55
  54.3 3.4 %fusion.6 = f32[384,1408]{1,0:T(8,128)S(1)} fusion(bf16[1,1024,1408]{2,1,0:T(8,128)(2,1)} %all-gather.9.cloned.1.call-done, bf16[192,1024]{1,0:T(8,128)(2,1)} %copy-done.17, bf16[192,1024]{1,0:T(8,128)(2,1)} %bitcast.118), kind=kOutput, calls=%fused_computation.9 | convolution fusion | flops 1108869120 | bytes 5832704 | tf_op jit(solution)/shard_map/dot_general | solution.py:14
  57.7 1.0 slice.142
  58.7 39.1 %all-gather.7.cloned.1.call-done = bf16[1,1024,1408]{2,1,0:T(8,128)(2,1)} async-done(((bf16[1,256,1408]{2,1,0:T(8,128)(2,1)}), bf16[1,1024,1408]{2,1,0:T(8,128)(2,1)}) %all-gather.7.cloned.1.call-update) | async-done | bytes 2883600 | tf_op jit(solution)/shard_map/all_gather | solution.py:55
  97.8 3.4 %fusion.10 = f32[384,1408]{1,0:T(8,128)S(1)} fusion(bf16[1,1024,1408]{2,1,0:T(8,128)(2,1)} %all-gather.7.cloned.1.call-done, bf16[192,1024]{1,0:T(8,128)(2,1)} %copy-done.17, bf16[192,1024]{1,0:T(8,128)(2,1)} %bitcast.119), kind=kOutput, calls=%fused_computation.13 | convolution fusion | flops 1108869120 | bytes 5832704 | tf_op jit(solution)/shard_map/dot_general | solution.py:14
  101.4 1.9 collective-permute-done.1
  103.3 2.5 multiply_convert_fusion.2
  105.9 35.4 %all-gather.11.cloned.1.call-done = bf16[1,1024,1408]{2,1,0:T(8,128)(2,1)} async-done(((bf16[1,256,1408]{2,1,0:T(8,128)(2,1)}), bf16[1,1024,1408]{2,1,0:T(8,128)(2,1)}) %all-gather.11.cloned.1.call-update) | async-done | bytes 2883600 | tf_op jit(solution)/shard_map/all_gather | solution.py:55
  141.4 0.8 copy-done.12
  142.2 3.4 fusion.14
  145.7 1.7 collective-permute-done.4
  147.4 1.0 pad_maximum_fusion.7
  148.4 4.6 %all-to-all-start.1 = ((bf16[4,2,48,1024]{3,2,1,0:T(8,128)(2,1)}), bf16[4,2,48,1024]{3,2,1,0:T(8,128)(2,1)S(1)}, u32[]{:S(2)}, u32[]{:S(2)}) async-start(bf16[4,2,48,1024]{3,2,1,0:T(8,128)(2,1)} %pad_maximum_fusion.7), calls=%async_computation.1 | async-start | bytes 1572864 | tf_op jit(solution)/shard_map/all_to_all | solution.py:78
  153.0 20.4 %all-to-all-done.1 = bf16[4,2,48,1024]{3,2,1,0:T(8,128)(2,1)S(1)} async-done(((bf16[4,2,48,1024]{3,2,1,0:T(8,128)(2,1)}), bf16[4,2,48,1024]{3,2,1,0:T(8,128)(2,1)S(1)}, u32[]{:S(2)}, u32[]{:S(2)}) %all-to-all-start.1) | async-done | bytes 786464 | tf_op jit(solution)/shard_map/all_to_all | solution.py:78
  174.1 0.6 select_reduce_fusion.1
  174.7 0.3 convolution_convert_fusion.7
  175.1 0.3 convolution_convert_fusion.8
  175.5 22.2 %all_to_all.21 = bf16[4,2,48,1024]{3,2,1,0:T(8,128)(2,1)S(1)} all-to-all(bf16[4,2,48,1024]{3,2,1,0:T(8,128)(2,1)S(1)} %pad_maximum_fusion.8), channel_id=1, replica_groups=mesh['expert'=4,'fsdp'=8] {'expert'}, dimensions={0} | all-to-all | bytes 1572864 | tf_op jit(solution)/shard_map/all_to_all | solution.py:78
  197.9 1.7 collective-permute-done.5
  199.6 4.4 %convolution_convert_fusion = bf16[1024,1408]{1,0:T(8,128)(2,1)} fusion(bf16[192,1408]{1,0:T(8,128)(2,1)S(1)} %copy-done.13, bf16[192,1408]{1,0:T(8,128)(2,1)} %multiply_convert_fusion.2, bf16[192,1024]{1,0:T(8,128)(2,1)S(1)} %collective-permute-done.5, bf16[192,1024]{1,0:T(8,128)(2,1)S(1)} %bitcast.122), kind=kOutput, calls=%fused_computation | convolution fusion | flops 1112473600 | bytes 4751360 | tf_op jit(solution)/shard_map/dot_general | solution.py:14
  204.3 3.3 fusion
  207.9 1.8 collective-permute-done.6
  209.8 2.6 multiply_convert_fusion.1
  212.4 1.8 collective-permute-done.7
  214.2 0.8 copy-done.14
  215.0 3.3 convolution_convert_fusion.2
  218.4 1.0 copy-done.7
  219.6 1.8 collective-permute-done.8
  221.4 0.8 copy-done.16
  222.2 3.4 convolution_convert_fusion.1
  225.6 3.5 %fusion.4 = f32[384,1024]{1,0:T(8,128)S(1)} fusion(bf16[1,1024,1408]{2,1,0:T(8,128)(2,1)} %all-gather.9.cloned.1.call-done, bf16[192,1408]{1,0:T(8,128)(2,1)} %copy-done.16, bf16[192,1408]{1,0:T(8,128)(2,1)S(1)} %copy-done.7), kind=kOutput, calls=%fused_computation.7 | convolution fusion | flops 1109458944 | bytes 5537792 | tf_op jit(solution)/shard_map/dot_general | solution.py:14
  229.2 1.4 add_convert_fusion
  230.9 1.5 collective-permute-done.9
  232.5 1.0 pad_maximum_fusion.10
  233.4 3.7 %all-to-all-start.3 = ((bf16[4,2,48,1024]{3,2,1,0:T(8,128)(2,1)}), bf16[4,2,48,1024]{3,2,1,0:T(8,128)(2,1)S(1)}, u32[]{:S(2)}, u32[]{:S(2)}) async-start(bf16[4,2,48,1024]{3,2,1,0:T(8,128)(2,1)} %pad_maximum_fusion.10), calls=%async_computation.3 | async-start | bytes 1572864 | tf_op jit(solution)/shard_map/all_to_all | solution.py:78
  237.5 0.3 broadcast_select_fusion.7
  237.8 0.4 reshape.274
  238.2 0.4 reshape.275
  238.5 0.7 pad_maximum_fusion.3
  239.3 1.6 copy.47
  240.9 1.6 reshape.276
  242.5 15.1 %all-to-all-done.3 = bf16[4,2,48,1024]{3,2,1,0:T(8,128)(2,1)S(1)} async-done(((bf16[4,2,48,1024]{3,2,1,0:T(8,128)(2,1)}), bf16[4,2,48,1024]{3,2,1,0:T(8,128)(2,1)S(1)}, u32[]{:S(2)}, u32[]{:S(2)}) %all-to-all-start.3) | async-done | bytes 786464 | tf_op jit(solution)/shard_map/all_to_all | solution.py:78
  257.7 0.3 convolution_convert_fusion.3
  258.0 0.3 broadcast_select_fusion.5
  258.4 0.4 reshape.278
  258.8 0.4 reshape.279
  259.1 0.7 pad_maximum_fusion.4
  259.9 1.6 copy.53
  261.5 1.6 reshape.280
  263.1 2.3 bitcast_convert_fusion
  265.4 23.3 %reduce-scatter.4.cloned.1.call-done = bf16[256,1408]{1,0:T(8,128)(2,1)} async-done(((bf16[1024,1408]{1,0:T(8,128)(2,1)}), bf16[256,1408]{1,0:T(8,128)(2,1)}) %reduce-scatter.4.cloned.1.call-update) | async-done | bytes 720912 | tf_op jit(solution)/shard_map/reduce_scatter | solution.py:58
  288.7 2.3 bitcast_convert_fusion.2
  291.0 42.4 %reduce-scatter.6.cloned.1.call-done = bf16[256,1408]{1,0:T(8,128)(2,1)} async-done(((bf16[1024,1408]{1,0:T(8,128)(2,1)}), bf16[256,1408]{1,0:T(8,128)(2,1)}) %reduce-scatter.6.cloned.1.call-update) | async-done | bytes 720912 | tf_op jit(solution)/shard_map/reduce_scatter | solution.py:58
  333.4 2.3 bitcast_convert_fusion.1
  (76 shorter events, 3.5 us)
Async XLA Ops:
  7.2 2.3 copy-start.9
  7.2 2.5 copy-start.6
  7.2 47.1 %all-gather.9.cloned.1.call-start = ((), (), s32[]{:S(2)}) async-start(), calls=%async_computation.11 | async-start | bytes 3604480 | tf_op jit(solution)/shard_map/all_gather | solution.py:55
  7.9 89.9 %all-gather.7.cloned.1.call-start = ((), (), s32[]{:S(2)}) async-start(), calls=%async_computation.10 | async-start | bytes 3604480 | tf_op jit(solution)/shard_map/all_gather | solution.py:55
  8.7 132.7 %all-gather.11.cloned.1.call-start = ((), (), s32[]{:S(2)}) async-start(), calls=%async_computation.12 | async-start | bytes 3604480 | tf_op jit(solution)/shard_map/all_gather | solution.py:55
  39.7 1.7 collective-permute-start
  41.4 12.8 %copy-start.17 = (bf16[192,1024]{1,0:T(8,128)(2,1)}, bf16[192,1024]{1,0:T(8,128)(2,1)S(1)}, u32[]{:S(2)}) copy-start(bf16[192,1024]{1,0:T(8,128)(2,1)S(1)} %collective-permute-done) | copy-start | bytes 1179652
  57.7 45.6 %copy-start = (f32[384,1408]{1,0:T(8,128)}, f32[384,1408]{1,0:T(8,128)S(1)}, u32[]{:S(2)}) copy-start(f32[384,1408]{1,0:T(8,128)S(1)} %fusion.6) | copy-start | bytes 6488068
  58.7 42.7 %collective-permute-start.2 = (bf16[192,1408]{1,0:T(8,128)(2,1)}, bf16[192,1408]{1,0:T(8,128)(2,1)}, u32[]{:S(2)}, u32[]{:S(2)}) collective-permute-start(bf16[192,1408]{1,0:T(8,128)(2,1)} %slice.142), channel_id=1, source_target_pairs={{0,1},{1,0},{2,3},{3,2},{4,5},{5,4},{6,7},{7,6},{8,9},{9,8},{10,11... | collective-permute-start | bytes 1622024 | tf_op jit(solution)/shard_map/ppermute | solution.py:52
  101.3 4.5 %copy-start.2 = (f32[384,1408]{1,0:T(8,128)}, f32[384,1408]{1,0:T(8,128)S(1)}, u32[]{:S(2)}) copy-start(f32[384,1408]{1,0:T(8,128)S(1)} %fusion.10) | copy-start | bytes 6488068
  101.3 2.0 collective-permute-start.1
  103.3 2.5 copy-start.4
  105.8 35.6 %collective-permute-start.3 = (bf16[192,1408]{1,0:T(8,128)(2,1)}, bf16[192,1408]{1,0:T(8,128)(2,1)S(1)}, u32[]{:S(2)}, u32[]{:S(2)}) collective-permute-start(bf16[192,1408]{1,0:T(8,128)(2,1)} %multiply_convert_fusion.2), channel_id=1, source_target_pairs={{0,1},{1,0},{2,3},{3,2},{4,5},{5,4},{6,7},{7,6},{8,9},{9,8},{10,11... | collective-permute-start | bytes 1622024 | tf_op jit(solution)/shard_map/ppermute | solution.py:52
  141.4 0.8 copy-start.12
  145.6 1.8 collective-permute-start.4
  147.4 5.6 %copy-start.10 = (bf16[256,6]{0,1:T(8,128)(2,1)S(1)}, bf16[256,6]{0,1:T(8,128)(2,1)}, u32[]{:S(2)}) copy-start(bf16[256,6]{0,1:T(8,128)(2,1)} %param.9) | copy-start | bytes 9220
  148.4 25.0 %all-to-all-start.1 = ((bf16[4,2,48,1024]{3,2,1,0:T(8,128)(2,1)}), bf16[4,2,48,1024]{3,2,1,0:T(8,128)(2,1)S(1)}, u32[]{:S(2)}, u32[]{:S(2)}) async-start(bf16[4,2,48,1024]{3,2,1,0:T(8,128)(2,1)} %pad_maximum_fusion.7), calls=%async_computation.1 | async-start | bytes 1572864 | tf_op jit(solution)/shard_map/all_to_all | solution.py:78
  153.0 110.2 %reduce-scatter.8.cloned.1.call-start = ((), (), s32[]{:S(2)}) async-start(), calls=%async_computation.9 | async-start | bytes 3604480 | tf_op jit(solution)/shard_map/reduce_scatter | solution.py:58
  175.5 24.1 %copy-start.13 = (bf16[192,1408]{1,0:T(8,128)(2,1)S(1)}, bf16[192,1408]{1,0:T(8,128)(2,1)}, u32[]{:S(2)}) copy-start(bf16[192,1408]{1,0:T(8,128)(2,1)} %copy-done.12) | copy-start | bytes 1622020
  197.8 1.8 collective-permute-start.5
  204.0 5.7 %copy-start.5 = (bf16[192,1408]{1,0:T(8,128)(2,1)S(1)}, bf16[192,1408]{1,0:T(8,128)(2,1)}, u32[]{:S(2)}) copy-start(bf16[192,1408]{1,0:T(8,128)(2,1)} %copy-done.4) | copy-start | bytes 1622020
  204.1 84.6 %reduce-scatter.4.cloned.1.call-start = ((), (), s32[]{:S(2)}) async-start(), calls=%async_computation.7 | async-start | bytes 3604480 | tf_op jit(solution)/shard_map/reduce_scatter | solution.py:58
  204.3 5.5 %copy-start.1 = (f32[384,1408]{1,0:T(8,128)S(1)}, f32[384,1408]{1,0:T(8,128)}, u32[]{:S(2)}) copy-start(f32[384,1408]{1,0:T(8,128)} %copy-done) | copy-start | bytes 6488068
  204.3 5.5 %copy-start.3 = (f32[384,1408]{1,0:T(8,128)S(1)}, f32[384,1408]{1,0:T(8,128)}, u32[]{:S(2)}) copy-start(f32[384,1408]{1,0:T(8,128)} %copy-done.2) | copy-start | bytes 6488068
  207.7 7.3 %copy-start.8 = (bf16[4,1,48,1024]{3,2,1,0:T(8,128)(2,1)S(1)}, bf16[4,1,48,1024]{3,2,1,0:T(8,128)(2,1)}, u32[]{:S(2)}) copy-start(bf16[4,1,48,1024]{3,2,1,0:T(8,128)(2,1)} %get-tuple-element.28) | copy-start | bytes 1179652
  207.7 7.3 %copy-start.18 = (bf16[192,1024]{1,0:T(8,128)(2,1)S(1)}, bf16[192,1024]{1,0:T(8,128)(2,1)}, u32[]{:S(2)}) copy-start(bf16[192,1024]{1,0:T(8,128)(2,1)} %copy-done.17) | copy-start | bytes 1179652
  207.7 2.0 collective-permute-start.6
  212.3 1.9 collective-permute-start.7
  214.2 0.8 copy-start.14
  218.4 1.0 copy-start.7
  218.4 115.0 %reduce-scatter.6.cloned.1.call-start = ((), (), s32[]{:S(2)}) async-start(), calls=%async_computation.8 | async-start | bytes 3604480 | tf_op jit(solution)/shard_map/reduce_scatter | solution.py:58
  219.4 1.9 collective-permute-start.8
  221.4 0.8 copy-start.16
  225.6 3.6 %copy-start.11 = (bf16[1,1024,1408]{2,1,0:T(8,128)(2,1)S(1)}, bf16[1,1024,1408]{2,1,0:T(8,128)(2,1)}, u32[]{:S(2)}) copy-start(bf16[1,1024,1408]{2,1,0:T(8,128)(2,1)} %all-gather.7.cloned.1.call-done) | copy-start | bytes 8650756
  225.6 3.6 %copy-start.15 = (bf16[192,1408]{1,0:T(8,128)(2,1)S(1)}, bf16[192,1408]{1,0:T(8,128)(2,1)}, u32[]{:S(2)}) copy-start(bf16[192,1408]{1,0:T(8,128)(2,1)} %copy-done.14) | copy-start | bytes 1622020
  230.7 1.8 collective-permute-start.9
  233.4 24.2 %all-to-all-start.3 = ((bf16[4,2,48,1024]{3,2,1,0:T(8,128)(2,1)}), bf16[4,2,48,1024]{3,2,1,0:T(8,128)(2,1)S(1)}, u32[]{:S(2)}, u32[]{:S(2)}) async-start(bf16[4,2,48,1024]{3,2,1,0:T(8,128)(2,1)} %pad_maximum_fusion.10), calls=%async_computation.3 | async-start | bytes 1572864 | tf_op jit(solution)/shard_map/all_to_all | solution.py:78
Sparse Core Ops, SparseCore 0:
  9.8 44.3 all-gather.8
  56.1 41.6 all-gather.6
  99.7 41.6 all-gather.10
  204.2 39.8 reduce-scatter.7
  246.9 41.7 reduce-scatter.3
  291.6 41.7 reduce-scatter.5

commit v2 on v1

--- a/solution.py
+++ b/solution.py
@@ -1,6 +1,10 @@
+import functools
+
 import jax
 import jax.numpy as jnp
 from jax import lax
+from jax.experimental import pallas as pl
+from jax.experimental.pallas import tpu as pltpu
 from jax.sharding import PartitionSpec as P
 
 EXPERTS = 64
@@ -12,6 +16,207 @@
 
 def dot(a, b, dims):
     return lax.dot_general(a, b, (dims, ((), ())), preferred_element_type=F32)
+
+
+MESH = pl.DeviceIdType.MESH
+HBM = pl.BlockSpec(memory_space=pltpu.MemorySpace.HBM)
+VMEM = pl.BlockSpec(memory_space=pltpu.MemorySpace.VMEM)
+
+
+class Place:
+    def __init__(self, groups):
+        self.groups = groups
+        self.e = lax.axis_index("expert")
+        f = lax.axis_index("fsdp")
+        self.f = f
+        self.chip = f // 2
+        self.pair = f + 1 - 2 * (f % 2)
+        bit_x, bit_y = self.chip % 2, self.chip // 2
+        self.to_x, self.to_y = f + 2 - 4 * bit_x, f + 4 - 8 * bit_y
+        self.chip_x, self.chip_y = self.chip + 1 - 2 * bit_x, self.chip + 2 - 4 * bit_y
+        self.chip_far = 3 - self.chip
+
+    def barrier(self, rows):
+        sem = pltpu.get_barrier_semaphore()
+        peers = [(self.e, self.to_x), (self.e, self.to_y)]
+        if rows:
+            for step in range(self.groups):
+                there = (self.e + step) % self.groups
+                peers.append((there, self.pair))
+                if step:
+                    peers.append((there, self.f))
+        for peer in peers:
+            pl.semaphore_signal(sem, inc=1, device_id=peer, device_id_type=MESH)
+        pl.semaphore_wait(sem, len(peers))
+
+    def rows(self, src, dst, which, send, recv, local):
+        copies = []
+        for half in range(2):
+            for step in range(self.groups):
+                there = (self.e + step) % self.groups
+                if half == 0 and step == 0:
+                    copy = pltpu.make_async_copy(
+                        src.at[0, self.e], dst.at[0, self.e], local.at[which]
+                    )
+                else:
+                    copy = pltpu.make_async_remote_copy(
+                        src_ref=src.at[half, there],
+                        dst_ref=dst.at[half, self.e],
+                        send_sem=send.at[which, half, step],
+                        recv_sem=recv.at[which, half, step],
+                        device_id=(there, self.pair if half else self.f),
+                        device_id_type=MESH,
+                    )
+                copy.start()
+                copies.append(copy)
+        return copies
+
+    def send(self, src, dst, send, recv, index, to):
+        copy = pltpu.make_async_remote_copy(
+            src_ref=src,
+            dst_ref=dst,
+            send_sem=send.at[index],
+            recv_sem=recv.at[index],
+            device_id=(self.e, to),
+            device_id_type=MESH,
+        )
+        copy.start()
+        return copy
+
+
+def gather_kernel(groups, count, n_rows, *refs):
+    ws, xs = refs[:count], refs[count : count + n_rows]
+    refs = refs[count + n_rows :]
+    fulls, ins = refs[:count], refs[count : count + n_rows]
+    ws_send, ws_recv, ws_local, x_send, x_recv, x_local = refs[count + n_rows :]
+    at = Place(groups)
+    half = ws[0].shape[0] // 2
+    at.barrier(n_rows > 0)
+    pending, first = [], []
+    for j in range(n_rows):
+        pending += at.rows(xs[j], ins[j], j, x_send, x_recv, x_local)
+    for i in range(count):
+        mine = fulls[i].at[at.chip]
+        first.append(
+            (
+                at.send(ws[i], mine, ws_send, ws_recv, 4 * i, at.to_x),
+                at.send(ws[i], mine, ws_send, ws_recv, 4 * i + 1, at.to_y),
+            )
+        )
+        keep = pltpu.make_async_copy(ws[i], mine, ws_local.at[i])
+        keep.start()
+        pending.append(keep)
+    for i in range(count):
+        by_x, by_y = first[i]
+        by_x.wait_recv()
+        part = fulls[i].at[at.chip_x, pl.ds(0, half)]
+        pending.append(at.send(part, part, ws_send, ws_recv, 4 * i + 2, at.to_y))
+        by_y.wait_recv()
+        part = fulls[i].at[at.chip_y, pl.ds(half, half)]
+        pending.append(at.send(part, part, ws_send, ws_recv, 4 * i + 3, at.to_x))
+        by_x.wait_send()
+        by_y.wait_send()
+    for copy in pending:
+        copy.wait()
+
+
+def gather_call(groups, ws, xs):
+    count, n_rows = len(ws), len(xs)
+    dma = pltpu.SemaphoreType.DMA
+    return pl.pallas_call(
+        functools.partial(gather_kernel, groups, count, n_rows),
+        out_shape=[jax.ShapeDtypeStruct((4,) + w.shape, BF16) for w in ws]
+        + [jax.ShapeDtypeStruct(x.shape, BF16) for x in xs],
+        in_specs=[VMEM] * (count + n_rows),
+        out_specs=[HBM] * (count + n_rows),
+        scratch_shapes=[
+            dma((4 * count,)),
+            dma((4 * count,)),
+            dma((count,)),
+            dma((n_rows, 2, groups)),
+            dma((n_rows, 2, groups)),
+            dma((n_rows,)),
+        ],
+        compiler_params=pltpu.CompilerParams(
+            collective_id=0, has_side_effects=True, vmem_limit_bytes=24 * 2**20
+        ),
+    )(*ws, *xs)
+
+
+def scatter_kernel(groups, count, n_rows, *refs):
+    ts, xs = refs[:count], refs[count : count + n_rows]
+    refs = refs[count + n_rows :]
+    from_x, from_y = refs[:count], refs[count : 2 * count]
+    backs = refs[2 * count : 2 * count + n_rows]
+    refs = refs[2 * count + n_rows :]
+    far_x, far_y, sum_x, sum_y, t_send, t_recv, x_send, x_recv, x_local = refs
+    at = Place(groups)
+    half = far_x.shape[1]
+    top, low = pl.ds(0, half), pl.ds(half, half)
+    at.barrier(n_rows > 0)
+    pending, first = [], []
+    for i in range(count):
+        first.append(
+            (
+                at.send(ts[i].at[at.chip_far, top], far_x.at[i], t_send, t_recv, 6 * i, at.to_x),
+                at.send(
+                    ts[i].at[at.chip_far, low], far_y.at[i], t_send, t_recv, 6 * i + 1, at.to_y
+                ),
+            )
+        )
+        pending.append(
+            at.send(
+                ts[i].at[at.chip_x, top], from_x[i].at[top], t_send, t_recv, 6 * i + 2, at.to_x
+            )
+        )
+        pending.append(
+            at.send(
+                ts[i].at[at.chip_y, low], from_y[i].at[low], t_send, t_recv, 6 * i + 3, at.to_y
+            )
+        )
+    for j in range(n_rows):
+        pending += at.rows(xs[j], backs[j], j, x_send, x_recv, x_local)
+    for i in range(count):
+        by_x, by_y = first[i]
+        by_x.wait_recv()
+        sum_y[i] = (ts[i][at.chip_y, top].astype(F32) + far_x[i].astype(F32)).astype(BF16)
+        pending.append(
+            at.send(sum_y.at[i], from_y[i].at[top], t_send, t_recv, 6 * i + 4, at.to_y)
+        )
+        by_y.wait_recv()
+        sum_x[i] = (ts[i][at.chip_x, low].astype(F32) + far_y[i].astype(F32)).astype(BF16)
+        pending.append(
+            at.send(sum_x.at[i], from_x[i].at[low], t_send, t_recv, 6 * i + 5, at.to_x)
+        )
+        by_x.wait_send()
+        by_y.wait_send()
+    for copy in pending:
+        copy.wait()
+
+
+def scatter_call(groups, ts, xs):
+    count, n_rows = len(ts), len(xs)
+    dma = pltpu.SemaphoreType.DMA
+    block, ff = ts[0].shape[1:]
+    piece = pltpu.VMEM((count, block // 2, ff), BF16)
+    return pl.pallas_call(
+        functools.partial(scatter_kernel, groups, count, n_rows),
+        out_shape=[jax.ShapeDtypeStruct((block, ff), BF16)] * (2 * count)
+        + [jax.ShapeDtypeStruct(x.shape, BF16) for x in xs],
+        in_specs=[VMEM] * (count + n_rows),
+        out_specs=[HBM] * (2 * count + n_rows),
+        scratch_shapes=[piece] * 4
+        + [
+            dma((6 * count,)),
+            dma((6 * count,)),
+            dma((n_rows, 2, groups)),
+            dma((n_rows, 2, groups)),
+            dma((n_rows,)),
+        ],
+        compiler_params=pltpu.CompilerParams(
+            collective_id=1, has_side_effects=True, vmem_limit_bytes=40 * 2**20
+        ),
+    )(*ts, *xs)
 
 
 def routes(expert_ids, gate_vals, groups):
@@ -78,19 +283,31 @@
         there = lax.all_to_all(packed, "expert", split_axis=0, concat_axis=0, tiled=True)
         return there[:, 0].reshape(rows, width // 2), there[:, 1].reshape(rows, width // 2)
 
-    full_gate, full_up, full_down = gather(w_gate), gather(w_up), gather(w_down)
+    square = columns == 8
     slot_is, place, pick, weighted = routes(expert_ids, gate_vals, groups)
     tok_mine, tok_other = halves(tokens)
     cot_mine, cot_other = halves(cotangent)
     first = ((0,), (0,))
-    row_mine, row_other = exchange(
-        dot(pick, tok_mine, first).astype(BF16), dot(pick, tok_other, first).astype(BF16)
-    )
-    og_mine, og_other = exchange(
-        dot(weighted, cot_mine, first).astype(BF16), dot(weighted, cot_other, first).astype(BF16)
-    )
-    row_in = jnp.concatenate([row_mine, swap(row_other)], axis=0)
-    out_grad = jnp.concatenate([og_mine, swap(og_other)], axis=0)
+    send_rows = [
+        dot(pick, tok_mine, first).astype(BF16),
+        dot(pick, tok_other, first).astype(BF16),
+        dot(weighted, cot_mine, first).astype(BF16),
+        dot(weighted, cot_other, first).astype(BF16),
+    ]
+    if square:
+        packed = [
+            jnp.stack(send_rows[i : i + 2]).reshape(2, groups, MOST, width // 2) for i in (0, 2)
+        ]
+        *full, row_in, out_grad = gather_call(groups, [w_gate[0], w_up[0], w_down[0]], packed)
+        full_gate, full_up, full_down = (w.reshape(width // 2, w.shape[2]) for w in full)
+        row_in = row_in.reshape(2 * rows, width // 2)
+        out_grad = out_grad.reshape(2 * rows, width // 2)
+    else:
+        full_gate, full_up, full_down = gather(w_gate), gather(w_up), gather(w_down)
+        row_mine, row_other = exchange(*send_rows[:2])
+        og_mine, og_other = exchange(*send_rows[2:])
+        row_in = jnp.concatenate([row_mine, swap(row_other)], axis=0)
+        out_grad = jnp.concatenate([og_mine, swap(og_other)], axis=0)
 
     def summed(x):
         return x[:rows] + swap(x[rows:].astype(BF16)).astype(F32)
@@ -108,14 +325,27 @@
     gate_grad = both(
         (hidden_grad * up_pre * sigmoid_g * (1.0 + gate_pre * (1.0 - sigmoid_g))).astype(BF16)
     )
-    grad_w_gate = scatter(dot(row_in, gate_grad, first))
     up_grad = both((hidden_grad * gate_pre * sigmoid_g).astype(BF16))
-    grad_w_up = scatter(dot(row_in, up_grad, first))
-
+    term_gate, term_up = dot(row_in, gate_grad, first), dot(row_in, up_grad, first)
     expert_out = dot(hidden, full_down, turned).astype(BF16)
-    out_mine, out_other = exchange(expert_out[:rows], swap(expert_out[rows:]))
     slot_grad = (dot(gate_grad, full_gate, turned) + dot(up_grad, full_up, turned)).astype(BF16)
-    sg_mine, sg_other = exchange(slot_grad[:rows], swap(slot_grad[rows:]))
+    if square:
+        terms = [t.astype(BF16).reshape(4, block, t.shape[1]) for t in (term_gate, term_up)]
+        back = [r.reshape(2, groups, MOST, width // 2) for r in (expert_out, slot_grad)]
+        gx, ux, gy, uy, out_back, sg_back = scatter_call(groups, terms, back)
+        chip = lax.axis_index("fsdp") // 2
+
+        def total(t, x, y):
+            own = lax.dynamic_index_in_dim(t, chip, 0, keepdims=False).astype(F32)
+            return (own + x.astype(F32) + y.astype(F32))[None]
+
+        grad_w_gate, grad_w_up = total(terms[0], gx, gy), total(terms[1], ux, uy)
+        out_mine, out_other = (out_back[i].reshape(rows, width // 2) for i in (0, 1))
+        sg_mine, sg_other = (sg_back[i].reshape(rows, width // 2) for i in (0, 1))
+    else:
+        grad_w_gate, grad_w_up = scatter(term_gate), scatter(term_up)
+        out_mine, out_other = exchange(expert_out[:rows], swap(expert_out[rows:]))
+        sg_mine, sg_other = exchange(slot_grad[:rows], swap(slot_grad[rows:]))
 
     output = whole_rows(
         dot(weighted, out_mine, plain).astype(BF16), dot(weighted, out_other, plain).astype(BF16)

time: 343 us -> 230 us (0.67)
  waiting for transfers between devices: 205 us -> 3.35 us
  Pallas kernels: 0 us -> 139 us
  blocking collectives: 48.5 us -> 0 us
  local copies, waits for them, and re-layouts: 15.6 us -> 28.1 us
  starting transfers between devices: 9.76 us -> 1.42 us
  matrix products: 33.1 us -> 28.5 us
    pallas_call x0 -> x2, Pallas kernels: none -> 139 us  [the longest x1 77.9 us: gather_call(): pl.pallas_call(functools.partial(gather_kernel, groups, count, n_rows), o...]
    all_gather x3 -> x0, waiting for transfers between devices: 87.4 us -> none  [gather(): lax.all_gather(w[0], 'fsdp', axis_index_groups=sides, axis=0, tiled=True)]
    reduce_scatter x3 -> x1, waiting for transfers between devices: 65.6 us -> 0.01 us  [scatter(): lax.psum_scatter(x.astype(BF16), 'fsdp', scatter_dimension=0, axis_index_...]
    all_to_all x2 -> x0, blocking collectives: 48.5 us -> none  [exchange(): lax.all_to_all(packed, 'expert', split_axis=0, concat_axis=0, tiled=True)]
    all_to_all x2 -> x0, waiting for transfers between devices: 35.5 us -> none  [exchange(): lax.all_to_all(packed, 'expert', split_axis=0, concat_axis=0, tiled=True)]
    ppermute x10 -> x6, waiting for transfers between devices: 14 us -> 3.33 us  [swap(): return lax.ppermute(x, 'fsdp', pairs)]
    all_to_all x2 -> x0, starting transfers between devices: 8.31 us -> none  [exchange(): lax.all_to_all(packed, 'expert', split_axis=0, concat_axis=0, tiled=True)]
    broadcast_in_dim x3 -> x1, other arithmetic: 6.91 us -> 2.3 us  [scatter(): lax.psum_scatter(x.astype(BF16), 'fsdp', scatter_dimension=0, axis_index_...]
  transfers between devices with their start and end apart: 18 -> 7, of which waited for: 15 -> 2; matrix products, arithmetic and copies ran while one was open for 14% -> 24% of each run, Pallas kernels for 0% -> 27%
where the time goes in v2:
time: 230 us
  Pallas kernels  139 us (60%)
  matrix products  28.5 us (12%)
  local copies, waits for them, and re-layouts  28.1 us (12%)
  between operations  14.7 us (6%)
  other arithmetic  14.4 us (6%)
  waiting for transfers between devices  3.35 us (1%)
    pallas_call x1, Pallas kernels, gather_call(): pl.pallas_call(functools.partial(gather_kernel, groups, count, n_rows), o...  77.9 us
    pallas_call x1, Pallas kernels, scatter_call(): pl.pallas_call(functools.partial(scatter_kernel, groups, count, n_rows),...  61.2 us
    dot_general x20, matrix products, dot(): return lax.dot_general(a, b, (dims, ((), ())), preferred_element_type=F32)  28.5 us
    unnamed x74, local copies, waits for them, and re-layouts  7.3 us
    reshape x2, local copies, waits for them, and re-layouts, whole_rows(): return jnp.concatenate([even, odd], axis=2).reshape(-1, width)  5.22 us
    concatenate x2, local copies, waits for them, and re-layouts, whole_rows(): return jnp.concatenate([even, odd], axis=2).reshape(-1, width)  5.18 us
  transfers between devices with their start and end apart: 7, of which 2 were waited for; matrix products, arithmetic and copies ran while one was open for 24% of the time, Pallas kernels for 27%

profile of v2, /device:TPU:0, one launch (start us, length us, event | category | flops | bytes accessed | tf_op | source)
XLA Modules:
  0.0 229.5 jit_solution(10207940272788538508)
XLA Ops:
  7.2 0.7 fusion.8
  8.0 0.2 convolution_convert_fusion.12
  8.1 0.7 convert_element_type.120
  9.0 1.5 copy.34
  10.5 1.5 copy.35
  12.0 0.1 broadcast_select_fusion.1
  12.2 0.3 convolution_convert_fusion.8
  12.5 0.3 convolution_convert_fusion.9
  12.8 0.3 convolution_convert_fusion.10
  13.2 0.3 convolution_convert_fusion.11
  13.5 0.1 pad_maximum_fusion.6.refs_4_
  13.6 0.1 pad_maximum_fusion.5.refs_3_
  13.7 0.9 copy-done.2
  14.6 0.2 copy-done.3
  14.8 0.2 copy-done.4
  15.1 77.9 %shard_map.118 = (bf16[4,256,1408]{2,1,0:T(8,128)(2,1)S(1)}, bf16[4,256,1408]{2,1,0:T(8,128)(2,1)S(1)}, bf16[4,256,1408]{2,1,0:T(8,128)(2,1)S(1)}, bf16[2,4,48,1...) custom-call(bf16[256,1408]{1,0:T(8,128)(2,1)S(1)} %bitcast.81, bf16[256,1408]{1,0:T(8,128)(2,1)S(1)} %bitcast.82, ...), custom_call_target="tpu_custom_call" | custom-call | tf_op jit(solution)/shard_map/pallas_call | solution.py:126
  93.0 1.4 fusion.19
  94.4 0.1 slice.99
  94.5 0.1 collective-permute-start
  94.6 1.4 fusion.21
  96.0 0.1 slice.97
  96.0 0.5 collective-permute-start.2
  96.6 1.4 fusion.20
  98.0 0.1 slice.98
  98.1 0.1 collective-permute-start.1
  98.2 1.9 collective-permute-done.1
  100.1 1.6 multiply_convert_fusion
  101.6 0.1 collective-permute-start.5
  101.8 0.4 collective-permute-start.3
  102.1 1.4 collective-permute-done.5
  103.6 0.8 copy-done.34
  104.4 3.4 %convolution_convert_fusion = bf16[1024,1408]{1,0:T(8,128)(2,1)} fusion(bf16[384,1024]{1,0:T(8,128)(2,1)S(1)} %bitcast.95, bf16[192,1408]{1,0:T(8,128)(2,1)S(1)} %collective-permute-done.5, bf16[192,1408]{1,0:T(8,128)(2,1)S(1)} %get-tuple-element.28), kind=kOutput, calls=%fused_computation | convolution fusion | flops 1110900736 | bytes 4751360 | tf_op jit(solution)/shard_map/dot_general | solution.py:18
  107.8 0.2 collective-permute-start.4
  108.0 3.3 %convolution_convert_fusion.2 = bf16[1024,1408]{1,0:T(8,128)(2,1)S(1)} fusion(bf16[384,1024]{1,0:T(8,128)(2,1)} %bitcast.92, bf16[192,1408]{1,0:T(8,128)(2,1)} %collective-permute-done.3, bf16[192,1408]{1,0:T(8,128)(2,1)} %copy-done.24), kind=kOutput, calls=%fused_computation.2 | convolution fusion | flops 1110900736 | bytes 4751360 | tf_op jit(solution)/shard_map/dot_general | solution.py:18
  111.3 3.4 %convolution_convert_fusion.1 = bf16[1024,1408]{1,0:T(8,128)(2,1)S(1)} fusion(bf16[384,1024]{1,0:T(8,128)(2,1)S(1)} %bitcast.93, bf16[192,1408]{1,0:T(8,128)(2,1)} %collective-permute-done.4, bf16[192,1408]{1,0:T(8,128)(2,1)} %get-tuple-element.30), kind=kOutput, calls=%fused_computation.1 | convolution fusion | flops 1110900736 | bytes 4751360 | tf_op jit(solution)/shard_map/dot_general | solution.py:18
  114.8 1.4 convolution_convert_fusion.3
  116.2 1.4 copy-done.16
  117.6 2.8 %fusion.4 = f32[384,1024]{1,0:T(8,128)S(1)} fusion(bf16[1024,1408]{1,0:T(8,128)(2,1)S(1)} %bitcast.87, bf16[192,1408]{1,0:T(8,128)(2,1)} %collective-permute-done.4, bf16[192,1408]{1,0:T(8,128)(2,1)} %get-tuple-element.30), kind=kOutput, calls=%fused_computation.39 | convolution fusion | flops 1109458944 | bytes 5537792 | tf_op jit(solution)/shard_map/dot_general | solution.py:18
  120.4 2.5 %add_convert_fusion = bf16[384,1024]{1,0:T(8,128)(2,1)S(1)} fusion(f32[384,1024]{1,0:T(8,128)S(1)} %fusion.4, bf16[1024,1408]{1,0:T(8,128)(2,1)S(1)} %bitcast.85, bf16[192,1408]{1,0:T(8,128)(2,1)} %collective-permute-done.3, bf16[192,1408]{1,0:T(8,128)(2,1)S(1)} %copy-done.25), kind=kOutput, calls=%fused_computation.3 | convolution fusion | flops 1110245376 | bytes 6324224 | tf_op jit(solution)/shard_map/dot_general | solution.py:18
  122.9 61.2 %shard_map.119 = (bf16[256,1408]{1,0:T(8,128)(2,1)S(1)}, bf16[256,1408]{1,0:T(8,128)(2,1)S(1)}, bf16[256,1408]{1,0:T(8,128)(2,1)S(1)}, bf16[256,1408]{1,0:T(8,12...) custom-call(bf16[4,256,1408]{2,1,0:T(8,128)(2,1)S(1)} %bitcast.75, ...), custom_call_target="tpu_custom_call" | custom-call | tf_op jit(solution)/shard_map/pallas_call | solution.py:202
  184.1 0.1 fusion.18
  184.2 0.3 convolution_convert_fusion.6
  184.5 0.5 copy-done.22
  185.1 1.4 broadcast_select_fusion.7
  186.5 2.3 reshape.325
  188.8 2.2 reshape.326
  191.0 2.0 pad_maximum_fusion.3
  193.0 2.6 %copy.36 = bf16[256,4,2,256]{3,2,1,0:T(2,128)(2,1)} copy(bf16[256,4,2,256]{3,1,0,2:T(4,128)(2,1)S(1)} %pad_maximum_fusion.3) | data formatting | bytes 2097152 | tf_op jit(solution)/shard_map/concatenate | solution.py:276
  195.6 2.6 %reshape.327 = bf16[256,2048]{1,0:T(8,128)(2,1)} reshape(bf16[256,4,2,256]{3,2,1,0:T(2,128)(2,1)} %copy.36) | data formatting | bytes 2097152 | tf_op jit(solution)/shard_map/reshape | solution.py:276
  198.2 1.2 fusion.17
  199.4 0.3 convolution_convert_fusion.4
  199.7 1.3 broadcast_select_fusion.5
  201.1 2.3 reshape.328
  203.3 2.2 reshape.329
  205.5 2.0 pad_maximum_fusion.4
  207.5 2.6 %copy.37 = bf16[256,4,2,256]{3,2,1,0:T(2,128)(2,1)} copy(bf16[256,4,2,256]{3,1,0,2:T(4,128)(2,1)S(1)} %pad_maximum_fusion.4) | data formatting | bytes 2097152 | tf_op jit(solution)/shard_map/concatenate | solution.py:276
  210.1 2.6 %reshape.330 = bf16[256,2048]{1,0:T(8,128)(2,1)} reshape(bf16[256,4,2,256]{3,2,1,0:T(2,128)(2,1)} %copy.37) | data formatting | bytes 2097152 | tf_op jit(solution)/shard_map/reshape | solution.py:276
  212.8 1.5 fusion.22
  214.3 1.3 convolution_add_fusion
  215.6 0.1 select_reduce_fusion
  215.7 0.6 select_reduce_fusion.1
  216.3 2.6 %fusion.1 = f32[1,256,1408]{2,1,0:T(8,128)} fusion(bf16[256,1408]{1,0:T(8,128)(2,1)S(1)} %copy-done.12, bf16[256,1408]{1,0:T(8,128)(2,1)S(1)} %copy-done.10, bf16[4,256,1408]{2,1,0:T(8,128)(2,1)} %bitcast.78, s32[]{:T(128)S(6)} %select_n.142), kind=kLoop, calls=%fused_computation.6 | loop fusion | flops 1802240 | bytes 3604484 | tf_op jit(solution)/shard_map/broadcast_in_dim | solution.py:340
  218.9 1.4 fusion.3
  220.4 2.3 %bitcast_convert_fusion = f32[1,256,1408]{2,1,0:T(8,128)} fusion(bf16[256,1408]{1,0:T(8,128)(2,1)} %reduce-scatter.2.cloned.1.call-done), kind=kLoop, calls=%fused_computation.38 | loop fusion | flops 360448 | bytes 2162688 | tf_op jit(solution)/shard_map/broadcast_in_dim | solution.py:263
  (77 shorter events, 0.4 us)
Async XLA Ops:
  7.2 213.2 %reduce-scatter.2.cloned.1.call-start = ((), (), s32[]{:S(2)}) async-start(), calls=%async_computation.1 | async-start | bytes 3604480 | tf_op jit(solution)/shard_map/reduce_scatter | solution.py:263
  7.9 4.0 %copy-start.28 = (s32[256,6]{0,1:T(8,128)}, s32[256,6]{0,1:T(8,128)S(1)}, u32[]{:S(2)}) copy-start(s32[256,6]{0,1:T(8,128)S(1)} %fusion.8) | copy-start | bytes 18436
  8.0 4.0 %copy-start.32 = (pred[256,4]{0,1:T(4,128)(4,1)}, pred[256,4]{0,1:T(4,128)(4,1)S(1)}, u32[]{:S(2)}) copy-start(pred[256,4]{0,1:T(4,128)(4,1)S(1)} %fusion.6) | copy-start | bytes 3076
  8.1 3.8 %copy-start.30 = (s32[256,4]{0,1:T(4,128)}, s32[256,4]{0,1:T(4,128)S(1)}, u32[]{:S(2)}) copy-start(s32[256,4]{0,1:T(4,128)S(1)} %convolution_convert_fusion.12) | copy-start | bytes 12292
  12.1 1.4 copy-start.21
  13.5 1.1 copy-start.2
  13.5 1.3 copy-start.3
  13.5 1.5 copy-start.4
  93.0 1.6 copy-start.13
  93.0 3.0 %copy-start.17 = (bf16[4,256,1408]{2,1,0:T(8,128)(2,1)}, bf16[4,256,1408]{2,1,0:T(8,128)(2,1)S(1)}, u32[]{:S(2)}) copy-start(bf16[4,256,1408]{2,1,0:T(8,128)(2,1)S(1)} %get-tuple-element.19) | copy-start | bytes 8650756
  93.0 3.6 %copy-start.15 = (bf16[4,256,1408]{2,1,0:T(8,128)(2,1)}, bf16[4,256,1408]{2,1,0:T(8,128)(2,1)S(1)}, u32[]{:S(2)}) copy-start(bf16[4,256,1408]{2,1,0:T(8,128)(2,1)S(1)} %get-tuple-element.20) | copy-start | bytes 8650756
  93.0 3.6 %copy-start.19 = (bf16[2,4,48,1024]{3,2,1,0:T(8,128)(2,1)}, bf16[2,4,48,1024]{3,2,1,0:T(8,128)(2,1)S(1)}, u32[]{:S(2)}) copy-start(bf16[2,4,48,1024]{3,2,1,0:T(8,128)(2,1)S(1)} %get-tuple-element.17) | copy-start | bytes 2359300
  94.5 3.7 %collective-permute-start = (bf16[192,1408]{1,0:T(8,128)(2,1)S(1)}, bf16[192,1408]{1,0:T(8,128)(2,1)S(1)}, u32[]{:S(2)}, u32[]{:S(2)}) collective-permute-start(bf16[192,1408]{1,0:T(8,128)(2,1)S(1)} %slice.99), channel_id=1, source_target_pairs={{0,1},{1,0},{2,3},{3,2},{4,5},{5,4},{6,7},{7,6},{8,9},{9,8},{10,11... | collective-permute-start | bytes 1622024 | tf_op jit(solution)/shard_map/ppermute | solution.py:257
  96.0 2.1 collective-permute-start.2
  98.1 2.0 collective-permute-start.1
  101.6 1.9 copy-start.26
  101.6 6.1 %copy-start.24 = (bf16[192,1408]{1,0:T(8,128)(2,1)}, bf16[192,1408]{1,0:T(8,128)(2,1)S(1)}, u32[]{:S(2)}) copy-start(bf16[192,1408]{1,0:T(8,128)(2,1)S(1)} %get-tuple-element.29) | copy-start | bytes 1622020
  101.6 1.9 collective-permute-start.5
  101.8 6.2 %collective-permute-start.3 = (bf16[192,1408]{1,0:T(8,128)(2,1)S(1)}, bf16[192,1408]{1,0:T(8,128)(2,1)}, u32[]{:S(2)}, u32[]{:S(2)}) collective-permute-start(bf16[192,1408]{1,0:T(8,128)(2,1)S(1)} %get-tuple-element.29), channel_id=1, source_target_pairs={{0,1},{1,0},{2,3},{3,2},{4,5},{5,4},{6,7},{7,6},{8,9},{9,8},{10,11... | collective-permute-start | bytes 1622024 | tf_op jit(solution)/shard_map/ppermute | solution.py:257
  103.6 0.8 copy-start.34
  107.8 3.5 %collective-permute-start.4 = (bf16[192,1408]{1,0:T(8,128)(2,1)}, bf16[192,1408]{1,0:T(8,128)(2,1)}, u32[]{:S(2)}, u32[]{:S(2)}) collective-permute-start(bf16[192,1408]{1,0:T(8,128)(2,1)} %get-tuple-element.30), channel_id=1, source_target_pairs={{0,1},{1,0},{2,3},{3,2},{4,5},{5,4},{6,7},{7,6},{8,9},{9,8},{10,11... | collective-permute-start | bytes 1622024 | tf_op jit(solution)/shard_map/ppermute | solution.py:257
  108.0 3.4 %copy-start.20 = (bf16[2,4,48,1024]{3,2,1,0:T(8,128)(2,1)S(1)}, bf16[2,4,48,1024]{3,2,1,0:T(8,128)(2,1)}, u32[]{:S(2)}) copy-start(bf16[2,4,48,1024]{3,2,1,0:T(8,128)(2,1)} %copy-done.19) | copy-start | bytes 2359300
  111.3 3.5 %copy-start.18 = (bf16[4,256,1408]{2,1,0:T(8,128)(2,1)S(1)}, bf16[4,256,1408]{2,1,0:T(8,128)(2,1)}, u32[]{:S(2)}) copy-start(bf16[4,256,1408]{2,1,0:T(8,128)(2,1)} %copy-done.17) | copy-start | bytes 8650756
  111.3 3.5 %copy-start.27 = (bf16[192,1408]{1,0:T(8,128)(2,1)S(1)}, bf16[192,1408]{1,0:T(8,128)(2,1)}, u32[]{:S(2)}) copy-start(bf16[192,1408]{1,0:T(8,128)(2,1)} %copy-done.26) | copy-start | bytes 1622020
  111.3 3.5 %copy-start.35 = (bf16[192,1408]{1,0:T(8,128)(2,1)S(1)}, bf16[192,1408]{1,0:T(8,128)(2,1)}, u32[]{:S(2)}) copy-start(bf16[192,1408]{1,0:T(8,128)(2,1)} %copy-done.34) | copy-start | bytes 1622020
  114.8 8.1 %copy-start = (bf16[1024,1408]{1,0:T(8,128)(2,1)}, bf16[1024,1408]{1,0:T(8,128)(2,1)S(1)}, u32[]{:S(2)}) copy-start(bf16[1024,1408]{1,0:T(8,128)(2,1)S(1)} %convolution_convert_fusion.1) | copy-start | bytes 8650756
  114.8 2.9 %copy-start.16 = (bf16[4,256,1408]{2,1,0:T(8,128)(2,1)S(1)}, bf16[4,256,1408]{2,1,0:T(8,128)(2,1)}, u32[]{:S(2)}) copy-start(bf16[4,256,1408]{2,1,0:T(8,128)(2,1)} %copy-done.15) | copy-start | bytes 8650756
  117.6 2.8 %copy-start.14 = (bf16[4,256,1408]{2,1,0:T(8,128)(2,1)S(1)}, bf16[4,256,1408]{2,1,0:T(8,128)(2,1)}, u32[]{:S(2)}) copy-start(bf16[4,256,1408]{2,1,0:T(8,128)(2,1)} %copy-done.13) | copy-start | bytes 8650756
  117.6 2.8 %copy-start.25 = (bf16[192,1408]{1,0:T(8,128)(2,1)S(1)}, bf16[192,1408]{1,0:T(8,128)(2,1)}, u32[]{:S(2)}) copy-start(bf16[192,1408]{1,0:T(8,128)(2,1)} %copy-done.24) | copy-start | bytes 1622020
  184.1 2.4 %copy-start.1 = (bf16[2,4,48,1024]{3,2,1,0:T(8,128)(2,1)}, bf16[2,4,48,1024]{3,2,1,0:T(8,128)(2,1)S(1)}, u32[]{:S(2)}) copy-start(bf16[2,4,48,1024]{3,2,1,0:T(8,128)(2,1)S(1)} %get-tuple-element.23) | copy-start | bytes 2359300
  184.1 2.4 %copy-start.5 = (bf16[256,1408]{1,0:T(8,128)(2,1)}, bf16[256,1408]{1,0:T(8,128)(2,1)S(1)}, u32[]{:S(2)}) copy-start(bf16[256,1408]{1,0:T(8,128)(2,1)S(1)} %get-tuple-element.24) | copy-start | bytes 2162692
  184.1 2.4 %copy-start.7 = (bf16[256,1408]{1,0:T(8,128)(2,1)}, bf16[256,1408]{1,0:T(8,128)(2,1)S(1)}, u32[]{:S(2)}) copy-start(bf16[256,1408]{1,0:T(8,128)(2,1)S(1)} %get-tuple-element.25) | copy-start | bytes 2162692
  184.1 2.4 %copy-start.9 = (bf16[256,1408]{1,0:T(8,128)(2,1)}, bf16[256,1408]{1,0:T(8,128)(2,1)S(1)}, u32[]{:S(2)}) copy-start(bf16[256,1408]{1,0:T(8,128)(2,1)S(1)} %get-tuple-element.26) | copy-start | bytes 2162692
  184.1 2.4 %copy-start.11 = (bf16[256,1408]{1,0:T(8,128)(2,1)}, bf16[256,1408]{1,0:T(8,128)(2,1)S(1)}, u32[]{:S(2)}) copy-start(bf16[256,1408]{1,0:T(8,128)(2,1)S(1)} %get-tuple-element.27) | copy-start | bytes 2162692
  184.2 0.9 copy-start.22
  184.2 2.3 %copy-start.23 = (bf16[1,4,48,1024]{3,2,1,0:T(8,128)(2,1)}, bf16[1,4,48,1024]{3,2,1,0:T(8,128)(2,1)S(1)}, u32[]{:S(2)}) copy-start(bf16[1,4,48,1024]{3,2,1,0:T(8,128)(2,1)S(1)} %get-tuple-element.42) | copy-start | bytes 1179652
  212.7 2.8 %copy-start.31 = (s32[256,4]{0,1:T(4,128)S(1)}, s32[256,4]{0,1:T(4,128)}, u32[]{:S(2)}) copy-start(s32[256,4]{0,1:T(4,128)} %copy-done.30) | copy-start | bytes 12292
  212.7 2.9 %copy-start.33 = (pred[256,4]{0,1:T(4,128)(4,1)S(1)}, pred[256,4]{0,1:T(4,128)(4,1)}, u32[]{:S(2)}) copy-start(pred[256,4]{0,1:T(4,128)(4,1)} %copy-done.32) | copy-start | bytes 3076
  212.7 2.9 %copy-start.29 = (s32[256,6]{0,1:T(8,128)S(1)}, s32[256,6]{0,1:T(8,128)}, u32[]{:S(2)}) copy-start(s32[256,6]{0,1:T(8,128)} %copy-done.28) | copy-start | bytes 18436
  212.7 3.6 %copy-start.10 = (bf16[256,1408]{1,0:T(8,128)(2,1)S(1)}, bf16[256,1408]{1,0:T(8,128)(2,1)}, u32[]{:S(2)}) copy-start(bf16[256,1408]{1,0:T(8,128)(2,1)} %copy-done.9) | copy-start | bytes 2162692
  212.7 3.5 %copy-start.12 = (bf16[256,1408]{1,0:T(8,128)(2,1)S(1)}, bf16[256,1408]{1,0:T(8,128)(2,1)}, u32[]{:S(2)}) copy-start(bf16[256,1408]{1,0:T(8,128)(2,1)} %copy-done.11) | copy-start | bytes 2162692
  216.3 2.7 %copy-start.6 = (bf16[256,1408]{1,0:T(8,128)(2,1)S(1)}, bf16[256,1408]{1,0:T(8,128)(2,1)}, u32[]{:S(2)}) copy-start(bf16[256,1408]{1,0:T(8,128)(2,1)} %copy-done.5) | copy-start | bytes 2162692
  216.3 2.7 %copy-start.8 = (bf16[256,1408]{1,0:T(8,128)(2,1)S(1)}, bf16[256,1408]{1,0:T(8,128)(2,1)}, u32[]{:S(2)}) copy-start(bf16[256,1408]{1,0:T(8,128)(2,1)} %copy-done.7) | copy-start | bytes 2162692
Sparse Core Ops, SparseCore 0:
  107.9 51.6 reduce-scatter.1

commit v3 on v2

--- a/solution.py
+++ b/solution.py
@@ -85,16 +85,15 @@
 
 
 def gather_kernel(groups, count, n_rows, *refs):
-    ws, xs = refs[:count], refs[count : count + n_rows]
+    ws, picks = refs[:count], refs[count : count + n_rows]
     refs = refs[count + n_rows :]
+    toks, refs = refs[:n_rows], refs[n_rows:]
     fulls, ins = refs[:count], refs[count : count + n_rows]
-    ws_send, ws_recv, ws_local, x_send, x_recv, x_local = refs[count + n_rows :]
+    xs, ws_send, ws_recv, ws_local, x_send, x_recv, x_local = refs[count + n_rows :]
     at = Place(groups)
     half = ws[0].shape[0] // 2
     at.barrier(n_rows > 0)
     pending, first = [], []
-    for j in range(n_rows):
-        pending += at.rows(xs[j], ins[j], j, x_send, x_recv, x_local)
     for i in range(count):
         mine = fulls[i].at[at.chip]
         first.append(
@@ -106,6 +105,17 @@
         keep = pltpu.make_async_copy(ws[i], mine, ws_local.at[i])
         keep.start()
         pending.append(keep)
+    block = ws[0].shape[0]
+    for j in range(n_rows):
+        for half_of in range(2):
+            odd = at.f % 2 if half_of == 0 else 1 - at.f % 2
+            for k in range(4):
+                cols = pl.ds(pl.multiple_of((2 * k + odd) * block, block), block)
+                part = dot(picks[j][...], toks[j][:, cols], ((0,), (0,))).astype(BF16)
+                xs[j, half_of, :, :, pl.ds(k * block, block)] = part.reshape(
+                    groups, MOST, block
+                )
+        pending += at.rows(xs.at[j], ins[j], j, x_send, x_recv, x_local)
     for i in range(count):
         by_x, by_y = first[i]
         by_x.wait_recv()
@@ -120,16 +130,18 @@
         copy.wait()
 
 
-def gather_call(groups, ws, xs):
-    count, n_rows = len(ws), len(xs)
+def gather_call(groups, ws, picks, toks):
+    count, n_rows = len(ws), len(toks)
+    shape = (2, groups, MOST, toks[0].shape[1] // 2)
     dma = pltpu.SemaphoreType.DMA
     return pl.pallas_call(
         functools.partial(gather_kernel, groups, count, n_rows),
         out_shape=[jax.ShapeDtypeStruct((4,) + w.shape, BF16) for w in ws]
-        + [jax.ShapeDtypeStruct(x.shape, BF16) for x in xs],
-        in_specs=[VMEM] * (count + n_rows),
+        + [jax.ShapeDtypeStruct(shape, BF16)] * n_rows,
+        in_specs=[VMEM] * (count + 2 * n_rows),
         out_specs=[HBM] * (count + n_rows),
         scratch_shapes=[
+            pltpu.VMEM((n_rows,) + shape, BF16),
             dma((4 * count,)),
             dma((4 * count,)),
             dma((count,)),
@@ -140,83 +152,91 @@
         compiler_params=pltpu.CompilerParams(
             collective_id=0, has_side_effects=True, vmem_limit_bytes=24 * 2**20
         ),
-    )(*ws, *xs)
-
-
-def scatter_kernel(groups, count, n_rows, *refs):
-    ts, xs = refs[:count], refs[count : count + n_rows]
-    refs = refs[count + n_rows :]
-    from_x, from_y = refs[:count], refs[count : 2 * count]
-    backs = refs[2 * count : 2 * count + n_rows]
-    refs = refs[2 * count + n_rows :]
-    far_x, far_y, sum_x, sum_y, t_send, t_recv, x_send, x_recv, x_local = refs
+    )(*ws, *picks, *toks)
+
+
+def scatter_kernel(groups, *refs):
+    row_in, out_grad, hidden, gate_grad, up_grad, w_gate, w_up, w_down = refs[:8]
+    owns, from_x, from_y, backs = refs[8:11], refs[11:14], refs[14:17], refs[17:19]
+    term, xs, far_x, far_y, sum_x, sum_y, t_send, t_recv, x_send, x_recv, x_local = refs[19:]
     at = Place(groups)
-    half = far_x.shape[1]
+    block = term.shape[2]
+    half = block // 2
     top, low = pl.ds(0, half), pl.ds(half, half)
-    at.barrier(n_rows > 0)
+    at.barrier(True)
     pending, first = [], []
-    for i in range(count):
+    factors = ((out_grad, hidden), (row_in, gate_grad), (row_in, up_grad))
+
+    def product(i, chip):
+        a, b = factors[i]
+        cols = pl.ds(pl.multiple_of(chip * block, block), block)
+        return dot(a[:, cols], b[...], ((0,), (0,))).astype(BF16)
+
+    def send(i, n, src, dst, to):
+        return at.send(src, dst, t_send, t_recv, 6 * i + n, to)
+
+    for i in range(3):
+        term[i, 0] = product(i, at.chip_far)
         first.append(
             (
-                at.send(ts[i].at[at.chip_far, top], far_x.at[i], t_send, t_recv, 6 * i, at.to_x),
-                at.send(
-                    ts[i].at[at.chip_far, low], far_y.at[i], t_send, t_recv, 6 * i + 1, at.to_y
-                ),
+                send(i, 0, term.at[i, 0, top], far_x.at[i], at.to_x),
+                send(i, 1, term.at[i, 0, low], far_y.at[i], at.to_y),
             )
         )
-        pending.append(
-            at.send(
-                ts[i].at[at.chip_x, top], from_x[i].at[top], t_send, t_recv, 6 * i + 2, at.to_x
-            )
-        )
-        pending.append(
-            at.send(
-                ts[i].at[at.chip_y, low], from_y[i].at[low], t_send, t_recv, 6 * i + 3, at.to_y
-            )
-        )
-    for j in range(n_rows):
-        pending += at.rows(xs[j], backs[j], j, x_send, x_recv, x_local)
-    for i in range(count):
+        term[i, 1] = product(i, at.chip_x)
+        pending.append(send(i, 2, term.at[i, 1, top], from_x[i].at[top], at.to_x))
+        term[i, 2] = product(i, at.chip_y)
+        pending.append(send(i, 3, term.at[i, 2, low], from_y[i].at[low], at.to_y))
+    turned = ((1,), (1,))
+    back = dot(hidden[...], w_down[...], turned).astype(BF16)
+    xs[0] = back.reshape(xs.shape[1:])
+    pending += at.rows(xs.at[0], backs[0], 0, x_send, x_recv, x_local)
+    back = dot(gate_grad[...], w_gate[...], turned) + dot(up_grad[...], w_up[...], turned)
+    xs[1] = back.astype(BF16).reshape(xs.shape[1:])
+    pending += at.rows(xs.at[1], backs[1], 1, x_send, x_recv, x_local)
+    for i in range(3):
         by_x, by_y = first[i]
         by_x.wait_recv()
-        sum_y[i] = (ts[i][at.chip_y, top].astype(F32) + far_x[i].astype(F32)).astype(BF16)
-        pending.append(
-            at.send(sum_y.at[i], from_y[i].at[top], t_send, t_recv, 6 * i + 4, at.to_y)
-        )
+        sum_y[i] = (term[i, 2, top].astype(F32) + far_x[i].astype(F32)).astype(BF16)
+        pending.append(send(i, 4, sum_y.at[i], from_y[i].at[top], at.to_y))
         by_y.wait_recv()
-        sum_x[i] = (ts[i][at.chip_x, low].astype(F32) + far_y[i].astype(F32)).astype(BF16)
-        pending.append(
-            at.send(sum_x.at[i], from_x[i].at[low], t_send, t_recv, 6 * i + 5, at.to_x)
-        )
+        sum_x[i] = (term[i, 1, low].astype(F32) + far_y[i].astype(F32)).astype(BF16)
+        pending.append(send(i, 5, sum_x.at[i], from_x[i].at[low], at.to_x))
+        owns[i][...] = product(i, at.chip)
         by_x.wait_send()
         by_y.wait_send()
     for copy in pending:
         copy.wait()
 
 
-def scatter_call(groups, ts, xs):
-    count, n_rows = len(ts), len(xs)
+def scatter_call(groups, block, row_in, out_grad, acts, ws):
     dma = pltpu.SemaphoreType.DMA
-    block, ff = ts[0].shape[1:]
-    piece = pltpu.VMEM((count, block // 2, ff), BF16)
+    ff = acts[0].shape[1]
+    shape = (2, groups, MOST, row_in.shape[1])
+    piece = pltpu.VMEM((3, block // 2, ff), BF16)
     return pl.pallas_call(
-        functools.partial(scatter_kernel, groups, count, n_rows),
-        out_shape=[jax.ShapeDtypeStruct((block, ff), BF16)] * (2 * count)
-        + [jax.ShapeDtypeStruct(x.shape, BF16) for x in xs],
-        in_specs=[VMEM] * (count + n_rows),
-        out_specs=[HBM] * (2 * count + n_rows),
-        scratch_shapes=[piece] * 4
-        + [
-            dma((6 * count,)),
-            dma((6 * count,)),
-            dma((n_rows, 2, groups)),
-            dma((n_rows, 2, groups)),
-            dma((n_rows,)),
+        functools.partial(scatter_kernel, groups),
+        out_shape=[jax.ShapeDtypeStruct((block, ff), BF16)] * 9
+        + [jax.ShapeDtypeStruct(shape, BF16)] * 2,
+        in_specs=[VMEM] * 8,
+        out_specs=[VMEM] * 3 + [HBM] * 8,
+        scratch_shapes=[
+            pltpu.VMEM((3, 3, block, ff), BF16),
+            pltpu.VMEM((2,) + shape, BF16),
+            piece,
+            piece,
+            piece,
+            piece,
+            dma((18,)),
+            dma((18,)),
+            dma((2, 2, groups)),
+            dma((2, 2, groups)),
+            dma((2,)),
         ],
         compiler_params=pltpu.CompilerParams(
-            collective_id=1, has_side_effects=True, vmem_limit_bytes=40 * 2**20
+            collective_id=1, has_side_effects=True, vmem_limit_bytes=48 * 2**20
         ),
-    )(*ts, *xs)
+    )(row_in, out_grad, *acts, *ws)
 
 
 def routes(expert_ids, gate_vals, groups):
@@ -264,16 +284,23 @@
             x.astype(BF16), "fsdp", scatter_dimension=0, axis_index_groups=sides, tiled=True
         ).astype(F32)[None]
 
+    def cut(x, odd):
+        return jnp.concatenate(
+            [x[:, (2 * k + odd) * block : (2 * k + odd + 1) * block] for k in range(columns // 2)],
+            axis=1,
+        )
+
     def halves(x):
-        cut = x.reshape(x.shape[0], columns // 2, 2, block)
-        even = cut[:, :, 0].reshape(x.shape[0], width // 2)
-        odd = cut[:, :, 1].reshape(x.shape[0], width // 2)
+        even, odd = cut(x, 0), cut(x, 1)
         return jnp.where(side == 0, even, odd), jnp.where(side == 0, odd, even)
 
     def whole_rows(mine, other):
-        even = jnp.where(side == 0, mine, other).reshape(-1, columns // 2, 1, block)
-        odd = jnp.where(side == 0, other, mine).reshape(-1, columns // 2, 1, block)
-        return jnp.concatenate([even, odd], axis=2).reshape(-1, width)
+        even, odd = jnp.where(side == 0, mine, other), jnp.where(side == 0, other, mine)
+        parts = []
+        for k in range(columns // 2):
+            here = slice(k * block, (k + 1) * block)
+            parts += [even[:, here], odd[:, here]]
+        return jnp.concatenate(parts, axis=1)
 
     def exchange(mine, other):
         packed = jnp.stack(
@@ -285,27 +312,18 @@
 
     square = columns == 8
     slot_is, place, pick, weighted = routes(expert_ids, gate_vals, groups)
-    tok_mine, tok_other = halves(tokens)
-    cot_mine, cot_other = halves(cotangent)
     first = ((0,), (0,))
-    send_rows = [
-        dot(pick, tok_mine, first).astype(BF16),
-        dot(pick, tok_other, first).astype(BF16),
-        dot(weighted, cot_mine, first).astype(BF16),
-        dot(weighted, cot_other, first).astype(BF16),
-    ]
     if square:
-        packed = [
-            jnp.stack(send_rows[i : i + 2]).reshape(2, groups, MOST, width // 2) for i in (0, 2)
-        ]
-        *full, row_in, out_grad = gather_call(groups, [w_gate[0], w_up[0], w_down[0]], packed)
+        *full, row_in, out_grad = gather_call(
+            groups, [w_gate[0], w_up[0], w_down[0]], [pick, weighted], [tokens, cotangent]
+        )
         full_gate, full_up, full_down = (w.reshape(width // 2, w.shape[2]) for w in full)
         row_in = row_in.reshape(2 * rows, width // 2)
         out_grad = out_grad.reshape(2 * rows, width // 2)
     else:
         full_gate, full_up, full_down = gather(w_gate), gather(w_up), gather(w_down)
-        row_mine, row_other = exchange(*send_rows[:2])
-        og_mine, og_other = exchange(*send_rows[2:])
+        row_mine, row_other = exchange(*halves(dot(pick, tokens, first).astype(BF16)))
+        og_mine, og_other = exchange(*halves(dot(weighted, cotangent, first).astype(BF16)))
         row_in = jnp.concatenate([row_mine, swap(row_other)], axis=0)
         out_grad = jnp.concatenate([og_mine, swap(og_other)], axis=0)
 
@@ -320,40 +338,40 @@
     up_pre = summed(dot(row_in, full_up, plain))
     sigmoid_g = jax.nn.sigmoid(gate_pre)
     hidden = both((gate_pre * sigmoid_g * up_pre).astype(BF16))
-    grad_w_down = scatter(dot(out_grad, hidden, first))
     hidden_grad = summed(dot(out_grad, full_down, plain))
     gate_grad = both(
         (hidden_grad * up_pre * sigmoid_g * (1.0 + gate_pre * (1.0 - sigmoid_g))).astype(BF16)
     )
     up_grad = both((hidden_grad * gate_pre * sigmoid_g).astype(BF16))
-    term_gate, term_up = dot(row_in, gate_grad, first), dot(row_in, up_grad, first)
-    expert_out = dot(hidden, full_down, turned).astype(BF16)
-    slot_grad = (dot(gate_grad, full_gate, turned) + dot(up_grad, full_up, turned)).astype(BF16)
     if square:
-        terms = [t.astype(BF16).reshape(4, block, t.shape[1]) for t in (term_gate, term_up)]
-        back = [r.reshape(2, groups, MOST, width // 2) for r in (expert_out, slot_grad)]
-        gx, ux, gy, uy, out_back, sg_back = scatter_call(groups, terms, back)
-        chip = lax.axis_index("fsdp") // 2
-
-        def total(t, x, y):
-            own = lax.dynamic_index_in_dim(t, chip, 0, keepdims=False).astype(F32)
-            return (own + x.astype(F32) + y.astype(F32))[None]
-
-        grad_w_gate, grad_w_up = total(terms[0], gx, gy), total(terms[1], ux, uy)
-        out_mine, out_other = (out_back[i].reshape(rows, width // 2) for i in (0, 1))
-        sg_mine, sg_other = (sg_back[i].reshape(rows, width // 2) for i in (0, 1))
+        got = scatter_call(
+            groups,
+            block,
+            row_in,
+            out_grad,
+            [hidden, gate_grad, up_grad],
+            [full_gate, full_up, full_down],
+        )
+        grad_w_down, grad_w_gate, grad_w_up = (
+            (got[i].astype(F32) + got[3 + i].astype(F32) + got[6 + i].astype(F32))[None]
+            for i in range(3)
+        )
+        outs, grads = ([r[i].reshape(rows, width // 2) for i in (0, 1)] for r in got[9:])
     else:
-        grad_w_gate, grad_w_up = scatter(term_gate), scatter(term_up)
-        out_mine, out_other = exchange(expert_out[:rows], swap(expert_out[rows:]))
-        sg_mine, sg_other = exchange(slot_grad[:rows], swap(slot_grad[rows:]))
-
-    output = whole_rows(
-        dot(weighted, out_mine, plain).astype(BF16), dot(weighted, out_other, plain).astype(BF16)
-    )
-    grad_tokens = whole_rows(
-        dot(pick, sg_mine, plain).astype(BF16), dot(pick, sg_other, plain).astype(BF16)
-    )
-    met = dot(cot_mine, out_mine, turned) + dot(cot_other, out_other, turned)
+        grad_w_down = scatter(dot(out_grad, hidden, first))
+        grad_w_gate = scatter(dot(row_in, gate_grad, first))
+        grad_w_up = scatter(dot(row_in, up_grad, first))
+        expert_out = dot(hidden, full_down, turned).astype(BF16)
+        slot_grad = (
+            dot(gate_grad, full_gate, turned) + dot(up_grad, full_up, turned)
+        ).astype(BF16)
+        outs = exchange(expert_out[:rows], swap(expert_out[rows:]))
+        grads = exchange(slot_grad[:rows], swap(slot_grad[rows:]))
+
+    slot_out = whole_rows(*outs)
+    output = dot(weighted, slot_out, plain).astype(BF16)
+    grad_tokens = dot(pick, whole_rows(*grads), plain).astype(BF16)
+    met = dot(cotangent, slot_out, turned)
     met = jnp.sum(jnp.where(place, met.reshape(place.shape), 0.0), axis=2)
     grad_gates = jnp.sum(jnp.where(slot_is, met[:, None, :], 0.0), axis=2)
     return (output, grad_tokens, grad_gates, grad_w_gate, grad_w_up, grad_w_down)

time: 230 us -> 189 us (0.82)
  local copies, waits for them, and re-layouts: 28.1 us -> 5.18 us
  matrix products: 28.5 us -> 7.6 us
  Pallas kernels: 139 us -> 156 us
  between operations: 14.7 us -> 1.03 us
    dot_general x20 -> x7, matrix products: 28.5 us -> 7.6 us  [dot(): return lax.dot_general(a, b, (dims, ((), ())), preferred_element_type=F32)]
    pallas_call x1, Pallas kernels: 61.2 us -> 78.8 us  [scatter_call(): pl.pallas_call(functools.partial(scatter_kernel, groups), out_shape=[jax....]
    reshape x6 -> x0, local copies, waits for them, and re-layouts: 14.2 us -> none  [the longest x2 5.22 us: whole_rows(): return jnp.concatenate([even, odd], axis=2).reshape(-1, width)]
    concatenate x2, local copies, waits for them, and re-layouts: 5.18 us -> 0.03 us  [whole_rows(): return jnp.concatenate(parts, axis=1)]
    broadcast_in_dim x3 -> x2, other arithmetic: 6.36 us -> 3.38 us  [on_device(): (got[i].astype(F32) + got[3 + i].astype(F32) + got[6 + i].astype(F32))[None]]
    unnamed x74 -> x36, local copies, waits for them, and re-layouts: 7.3 us -> 4.44 us
    concatenate x2 -> x3, other arithmetic: 3.96 us -> 6.32 us  [both(): return jnp.concatenate([x, swap(x)], axis=0)]
  transfers between devices with their start and end apart: 7 -> 6, of which waited for: 2 -> 2; matrix products, arithmetic and copies ran while one was open for 24% -> 4% of each run, Pallas kernels for 27% -> 0%
where the time goes in v3:
time: 189 us
  Pallas kernels  156 us (83%)
  other arithmetic  14.3 us (8%)
  matrix products  7.6 us (4%)
  local copies, waits for them, and re-layouts  5.18 us (3%)
  waiting for transfers between devices  2.75 us (1%)
    pallas_call x1, Pallas kernels, scatter_call(): pl.pallas_call(functools.partial(scatter_kernel, groups), out_shape=[jax....  78.8 us
    pallas_call x1, Pallas kernels, gather_call(): pl.pallas_call(functools.partial(gather_kernel, groups, count, n_rows), o...  77.6 us
    dot_general x7, matrix products, dot(): return lax.dot_general(a, b, (dims, ((), ())), preferred_element_type=F32)  7.6 us
    concatenate x3, other arithmetic, both(): return jnp.concatenate([x, swap(x)], axis=0)  6.32 us
    unnamed x36, local copies, waits for them, and re-layouts  4.44 us
  transfers between devices with their start and end apart: 6, of which 2 were waited for; matrix products, arithmetic and copies ran while one was open for 4% of the time, Pallas kernels for 0%

profile of v3, /device:TPU:0, one launch (start us, length us, event | category | flops | bytes accessed | tf_op | source)
XLA Modules:
  0.0 189.0 jit_solution(14454175701505581377)
XLA Ops:
  0.6 0.0 copy-start
  0.6 0.0 copy-start.4
  0.7 0.9 fusion.3
  1.5 0.2 convolution_convert_fusion.2
  1.7 0.1 copy.28
  1.9 0.1 copy.29
  2.1 0.1 eq.55
  2.1 0.7 convert_element_type.71
  2.9 0.1 copy.30
  3.0 0.1 fusion.6
  3.1 0.0 copy-done
  3.1 0.0 copy-done.4
  3.1 0.0 copy-start.7
  3.1 1.1 copy-done.7
  4.2 0.0 copy-start.8
  4.2 1.1 copy-done.8
  5.4 0.0 copy-start.9
  5.4 1.1 copy-done.9
  6.5 77.6 %shard_map.118 = (bf16[4,256,1408]{2,1,0:T(8,128)(2,1)S(1)}, bf16[4,256,1408]{2,1,0:T(8,128)(2,1)S(1)}, bf16[4,256,1408]{2,1,0:T(8,128)(2,1)S(1)}, bf16[2,4,48,1...) custom-call(bf16[256,1408]{1,0:T(8,128)(2,1)S(1)} %bitcast.48, bf16[256,1408]{1,0:T(8,128)(2,1)S(1)} %bitcast.49, ...), custom_call_target="tpu_custom_call" | custom-call | tf_op jit(solution)/shard_map/pallas_call | solution.py:137
  84.1 0.0 copy-start.2
  84.1 0.0 copy-start.1
  84.1 0.0 copy-start.5
  84.1 0.0 copy-start.3
  84.1 0.0 copy-start.6
  84.2 1.4 fusion.8
  85.5 0.2 copy-done.2
  85.7 0.1 slice.174
  85.8 0.1 collective-permute-start.1
  85.8 0.7 copy-done.1
  86.6 1.4 fusion.7
  87.9 0.0 copy-done.5
  87.9 0.1 slice.175
  88.0 0.1 collective-permute-start
  88.1 0.0 copy-done.3
  88.1 0.0 copy-done.6
  88.1 1.4 fusion.9
  89.5 0.1 slice.173
  89.6 0.5 collective-permute-start.3
  90.1 0.0 collective-permute-done.1
  90.1 0.0 collective-permute-done
  90.1 1.6 collective-permute-done.3
  91.7 0.8 multiply_convert_fusion
  92.5 0.4 collective-permute-start.5
  92.9 0.1 collective-permute-start.4
  93.0 0.4 collective-permute-start.2
  93.4 1.2 collective-permute-done.5
  94.6 2.1 %pad_maximum_fusion.2.refs_4_ = bf16[384,1408]{1,0:T(8,128)(2,1)} fusion(bf16[192,1408]{1,0:T(8,128)(2,1)} %collective-permute-done.5, bf16[192,1408]{1,0:T(8,128)(2,1)S(1)} %get-tuple-element.40), kind=kLoop, calls=%fused_computation.14 | loop fusion | flops 2162688 | bytes 2162688 | tf_op jit(solution)/shard_map/concatenate | solution.py:334
  96.7 0.0 collective-permute-done.4
  96.7 2.1 %pad_maximum_fusion.1.refs_3_ = bf16[384,1408]{1,0:T(8,128)(2,1)} fusion(bf16[192,1408]{1,0:T(8,128)(2,1)} %collective-permute-done.4, bf16[192,1408]{1,0:T(8,128)(2,1)S(1)} %get-tuple-element.41), kind=kLoop, calls=%fused_computation.13 | loop fusion | flops 2162688 | bytes 2162688 | tf_op jit(solution)/shard_map/concatenate | solution.py:334
  98.8 0.0 collective-permute-done.2
  98.8 2.1 %pad_maximum_fusion.refs_2_ = bf16[384,1408]{1,0:T(8,128)(2,1)} fusion(bf16[192,1408]{1,0:T(8,128)(2,1)} %collective-permute-done.2, bf16[192,1408]{1,0:T(8,128)(2,1)S(1)} %get-tuple-element.42), kind=kLoop, calls=%fused_computation.12 | loop fusion | flops 2162688 | bytes 2162688 | tf_op jit(solution)/shard_map/concatenate | solution.py:334
  100.9 78.8 %shard_map.119 = (bf16[256,1408]{1,0:T(8,128)(2,1)S(1)}, bf16[256,1408]{1,0:T(8,128)(2,1)S(1)}, bf16[256,1408]{1,0:T(8,128)(2,1)S(1)}, bf16[256,1408]{1,0:T(8,12...) custom-call(bf16[384,1024]{1,0:T(8,128)(2,1)} %bitcast.45, ...), custom_call_target="tpu_custom_call" | custom-call | tf_op jit(solution)/shard_map/pallas_call | solution.py:217
  179.7 1.5 broadcast_select_fusion
  181.4 1.4 convolution_convert_fusion.1
  182.8 0.5 fusion.10
  183.5 1.4 convolution_convert_fusion
  184.9 0.1 select_reduce_fusion
  185.0 0.6 select_reduce_fusion.1
  185.6 0.0 copy-start.10
  185.6 1.3 add_bitcast_fusion.2
  186.9 0.0 copy-done.10
  186.9 2.0 %add_bitcast_fusion = (f32[1,256,1408]{2,1,0:T(8,128)}, f32[1,256,1408]{2,1,0:T(8,128)}) fusion(bf16[256,1408]{1,0:T(8,128)(2,1)S(1)} %get-tuple-element.37, bf16[256,1408]{1,0:T(8,128)(2,1)S(1)} %get-tuple-element.36, bf16[256,1408]{1,0:T(8,128)(2,1)S(1)} %get-tuple-element.35, bf16[256,1408]{1,0:T(8,128)(2,1)S(1)} %copy-done.10, ...), kind=kLoop, calls=%fused_computation.2 | loop fusion | flops 3604480 | bytes 7208960 | tf_op jit(solution)/shard_map/broadcast_in_dim | solution.py:356
  (23 shorter events, 0.4 us)
Async XLA Ops:
  0.6 2.5 %copy-start = (bf16[256,2048]{1,0:T(8,128)(2,1)S(1)}, bf16[256,2048]{1,0:T(8,128)(2,1)}, u32[]{:S(2)}) copy-start(bf16[256,2048]{1,0:T(8,128)(2,1)} %refs_6_.1) | copy-start | bytes 3145732
  0.6 2.5 %copy-start.4 = (bf16[256,2048]{1,0:T(8,128)(2,1)S(1)}, bf16[256,2048]{1,0:T(8,128)(2,1)}, u32[]{:S(2)}) copy-start(bf16[256,2048]{1,0:T(8,128)(2,1)} %refs_5_.1) | copy-start | bytes 3145732
  3.1 1.1 copy-start.7
  4.2 1.1 copy-start.8
  5.4 1.1 copy-start.9
  84.1 1.6 copy-start.2
  84.1 2.4 %copy-start.1 = (bf16[4,256,1408]{2,1,0:T(8,128)(2,1)}, bf16[4,256,1408]{2,1,0:T(8,128)(2,1)S(1)}, u32[]{:S(2)}) copy-start(bf16[4,256,1408]{2,1,0:T(8,128)(2,1)S(1)} %get-tuple-element.24) | copy-start | bytes 8650756
  84.1 3.8 %copy-start.5 = (bf16[2,4,48,1024]{3,2,1,0:T(8,128)(2,1)}, bf16[2,4,48,1024]{3,2,1,0:T(8,128)(2,1)S(1)}, u32[]{:S(2)}) copy-start(bf16[2,4,48,1024]{3,2,1,0:T(8,128)(2,1)S(1)} %get-tuple-element.22) | copy-start | bytes 2359300
  84.1 4.0 %copy-start.3 = (bf16[4,256,1408]{2,1,0:T(8,128)(2,1)}, bf16[4,256,1408]{2,1,0:T(8,128)(2,1)S(1)}, u32[]{:S(2)}) copy-start(bf16[4,256,1408]{2,1,0:T(8,128)(2,1)S(1)} %get-tuple-element.26) | copy-start | bytes 8650756
  84.1 4.0 %copy-start.6 = (bf16[2,4,48,1024]{3,2,1,0:T(8,128)(2,1)}, bf16[2,4,48,1024]{3,2,1,0:T(8,128)(2,1)S(1)}, u32[]{:S(2)}) copy-start(bf16[2,4,48,1024]{3,2,1,0:T(8,128)(2,1)S(1)} %get-tuple-element.23) | copy-start | bytes 2359300
  85.8 4.4 %collective-permute-start.1 = (bf16[192,1408]{1,0:T(8,128)(2,1)S(1)}, bf16[192,1408]{1,0:T(8,128)(2,1)S(1)}, u32[]{:S(2)}, u32[]{:S(2)}) collective-permute-start(bf16[192,1408]{1,0:T(8,128)(2,1)S(1)} %slice.174), channel_id=1, source_target_pairs={{0,1},{1,0},{2,3},{3,2},{4,5},{5,4},{6,7},{7,6},{8,9},{9,8},{10,11... | collective-permute-start | bytes 1622024 | tf_op jit(solution)/shard_map/ppermute | solution.py:277
  88.0 2.1 %collective-permute-start = (bf16[192,1408]{1,0:T(8,128)(2,1)S(1)}, bf16[192,1408]{1,0:T(8,128)(2,1)S(1)}, u32[]{:S(2)}, u32[]{:S(2)}) collective-permute-start(bf16[192,1408]{1,0:T(8,128)(2,1)S(1)} %slice.175), channel_id=1, source_target_pairs={{0,1},{1,0},{2,3},{3,2},{4,5},{5,4},{6,7},{7,6},{8,9},{9,8},{10,11... | collective-permute-start | bytes 1622024 | tf_op jit(solution)/shard_map/ppermute | solution.py:277
  89.6 2.1 %collective-permute-start.3 = (bf16[192,1408]{1,0:T(8,128)(2,1)S(1)}, bf16[192,1408]{1,0:T(8,128)(2,1)S(1)}, u32[]{:S(2)}, u32[]{:S(2)}) collective-permute-start(bf16[192,1408]{1,0:T(8,128)(2,1)S(1)} %slice.173), channel_id=1, source_target_pairs={{0,1},{1,0},{2,3},{3,2},{4,5},{5,4},{6,7},{7,6},{8,9},{9,8},{10,11... | collective-permute-start | bytes 1622024 | tf_op jit(solution)/shard_map/ppermute | solution.py:277
  92.5 2.1 %collective-permute-start.5 = (bf16[192,1408]{1,0:T(8,128)(2,1)S(1)}, bf16[192,1408]{1,0:T(8,128)(2,1)}, u32[]{:S(2)}, u32[]{:S(2)}) collective-permute-start(bf16[192,1408]{1,0:T(8,128)(2,1)S(1)} %get-tuple-element.40), channel_id=1, source_target_pairs={{0,1},{1,0},{2,3},{3,2},{4,5},{5,4},{6,7},{7,6},{8,9},{9,8},{10,11... | collective-permute-start | bytes 1622024 | tf_op jit(solution)/shard_map/ppermute | solution.py:277
  92.9 3.8 %collective-permute-start.4 = (bf16[192,1408]{1,0:T(8,128)(2,1)S(1)}, bf16[192,1408]{1,0:T(8,128)(2,1)}, u32[]{:S(2)}, u32[]{:S(2)}) collective-permute-start(bf16[192,1408]{1,0:T(8,128)(2,1)S(1)} %get-tuple-element.41), channel_id=1, source_target_pairs={{0,1},{1,0},{2,3},{3,2},{4,5},{5,4},{6,7},{7,6},{8,9},{9,8},{10,11... | collective-permute-start | bytes 1622024 | tf_op jit(solution)/shard_map/ppermute | solution.py:277
  93.0 5.8 %collective-permute-start.2 = (bf16[192,1408]{1,0:T(8,128)(2,1)S(1)}, bf16[192,1408]{1,0:T(8,128)(2,1)}, u32[]{:S(2)}, u32[]{:S(2)}) collective-permute-start(bf16[192,1408]{1,0:T(8,128)(2,1)S(1)} %get-tuple-element.42), channel_id=1, source_target_pairs={{0,1},{1,0},{2,3},{3,2},{4,5},{5,4},{6,7},{7,6},{8,9},{9,8},{10,11... | collective-permute-start | bytes 1622024 | tf_op jit(solution)/shard_map/ppermute | solution.py:277
  185.6 1.3 copy-start.10

commit v4 on v3

--- a/solution.py
+++ b/solution.py
@@ -158,7 +158,8 @@
 def scatter_kernel(groups, *refs):
     row_in, out_grad, hidden, gate_grad, up_grad, w_gate, w_up, w_down = refs[:8]
     owns, from_x, from_y, backs = refs[8:11], refs[11:14], refs[14:17], refs[17:19]
-    term, xs, far_x, far_y, sum_x, sum_y, t_send, t_recv, x_send, x_recv, x_local = refs[19:]
+    term, xs, far_x, far_y, sum_x, sum_y, others = refs[19:26]
+    t_send, t_recv, x_send, x_recv, x_local, a_send, a_recv = refs[26:]
     at = Place(groups)
     block = term.shape[2]
     half = block // 2
@@ -166,16 +167,23 @@
     at.barrier(True)
     pending, first = [], []
     factors = ((out_grad, hidden), (row_in, gate_grad), (row_in, up_grad))
+    rows = hidden.shape[0]
+    swaps = [
+        at.send(act, others.at[i], a_send, a_recv, i, at.pair)
+        for i, (_, act) in enumerate(factors)
+    ]
 
     def product(i, chip):
         a, b = factors[i]
         cols = pl.ds(pl.multiple_of(chip * block, block), block)
-        return dot(a[:, cols], b[...], ((0,), (0,))).astype(BF16)
+        own = dot(a[pl.ds(0, rows), cols], b[...], ((0,), (0,)))
+        return (own + dot(a[pl.ds(rows, rows), cols], others[i], ((0,), (0,)))).astype(BF16)
 
     def send(i, n, src, dst, to):
         return at.send(src, dst, t_send, t_recv, 6 * i + n, to)
 
     for i in range(3):
+        swaps[i].wait()
         term[i, 0] = product(i, at.chip_far)
         first.append(
             (
@@ -188,11 +196,14 @@
         term[i, 2] = product(i, at.chip_y)
         pending.append(send(i, 3, term.at[i, 2, low], from_y[i].at[low], at.to_y))
     turned = ((1,), (1,))
-    back = dot(hidden[...], w_down[...], turned).astype(BF16)
-    xs[0] = back.reshape(xs.shape[1:])
+    for slot in range(2):
+        act = others[0] if slot else hidden[...]
+        xs[0, slot] = dot(act, w_down[...], turned).astype(BF16).reshape(xs.shape[2:])
     pending += at.rows(xs.at[0], backs[0], 0, x_send, x_recv, x_local)
-    back = dot(gate_grad[...], w_gate[...], turned) + dot(up_grad[...], w_up[...], turned)
-    xs[1] = back.astype(BF16).reshape(xs.shape[1:])
+    for slot in range(2):
+        g, u = (others[1], others[2]) if slot else (gate_grad[...], up_grad[...])
+        back = dot(g, w_gate[...], turned) + dot(u, w_up[...], turned)
+        xs[1, slot] = back.astype(BF16).reshape(xs.shape[2:])
     pending += at.rows(xs.at[1], backs[1], 1, x_send, x_recv, x_local)
     for i in range(3):
         by_x, by_y = first[i]
@@ -227,11 +238,14 @@
             piece,
             piece,
             piece,
+            pltpu.VMEM((3,) + acts[0].shape, BF16),
             dma((18,)),
             dma((18,)),
             dma((2, 2, groups)),
             dma((2, 2, groups)),
             dma((2,)),
+            dma((3,)),
+            dma((3,)),
         ],
         compiler_params=pltpu.CompilerParams(
             collective_id=1, has_side_effects=True, vmem_limit_bytes=48 * 2**20
@@ -337,12 +351,12 @@
     gate_pre = summed(dot(row_in, full_gate, plain))
     up_pre = summed(dot(row_in, full_up, plain))
     sigmoid_g = jax.nn.sigmoid(gate_pre)
-    hidden = both((gate_pre * sigmoid_g * up_pre).astype(BF16))
+    hidden = (gate_pre * sigmoid_g * up_pre).astype(BF16)
     hidden_grad = summed(dot(out_grad, full_down, plain))
-    gate_grad = both(
-        (hidden_grad * up_pre * sigmoid_g * (1.0 + gate_pre * (1.0 - sigmoid_g))).astype(BF16)
-    )
-    up_grad = both((hidden_grad * gate_pre * sigmoid_g).astype(BF16))
+    gate_grad = (
+        hidden_grad * up_pre * sigmoid_g * (1.0 + gate_pre * (1.0 - sigmoid_g))
+    ).astype(BF16)
+    up_grad = (hidden_grad * gate_pre * sigmoid_g).astype(BF16)
     if square:
         got = scatter_call(
             groups,
@@ -358,6 +372,7 @@
         )
         outs, grads = ([r[i].reshape(rows, width // 2) for i in (0, 1)] for r in got[9:])
     else:
+        hidden, gate_grad, up_grad = both(hidden), both(gate_grad), both(up_grad)
         grad_w_down = scatter(dot(out_grad, hidden, first))
         grad_w_gate = scatter(dot(row_in, gate_grad, first))
         grad_w_up = scatter(dot(row_in, up_grad, first))

time: 189 us -> 188 us (level)
  other arithmetic: 14.3 us -> 10.1 us
  local copies, waits for them, and re-layouts: 5.18 us -> 8.49 us
    concatenate x3 -> x0, other arithmetic: 6.32 us -> none  [both(): return jnp.concatenate([x, swap(x)], axis=0)]
    slice x3, local copies, waits for them, and re-layouts: 0.18 us -> 3.39 us  [summed(): return x[:rows] + swap(x[rows:].astype(BF16)).astype(F32)]
    convert_element_type x1, other arithmetic: 0.79 us -> 2.78 us  [on_device(): up_grad = (hidden_grad * gate_pre * sigmoid_g).astype(BF16)]
    unnamed x36 -> x48, local copies, waits for them, and re-layouts: 4.44 us -> 4.54 us
  transfers between devices with their start and end apart: 6 -> 3, of which waited for: 2 -> 1; matrix products, arithmetic and copies ran while one was open for 4% -> 2% of each run, Pallas kernels for 0% -> 0%
where the time goes in v4:
time: 188 us; the launch traced here: 187 us
  Pallas kernels  157 us (84%)
  other arithmetic  10.1 us (5%)
  local copies, waits for them, and re-layouts  8.49 us (5%)
  matrix products  7.6 us (4%)
  waiting for transfers between devices  2.26 us (1%)
    pallas_call x1, Pallas kernels, scatter_call(): pl.pallas_call(functools.partial(scatter_kernel, groups), out_shape=[jax....  79.8 us
    pallas_call x1, Pallas kernels, gather_call(): pl.pallas_call(functools.partial(gather_kernel, groups, count, n_rows), o...  77.6 us
    dot_general x7, matrix products, dot(): return lax.dot_general(a, b, (dims, ((), ())), preferred_element_type=F32)  7.6 us
    unnamed x48, local copies, waits for them, and re-layouts  4.54 us
  transfers between devices with their start and end apart: 3, of which 1 were waited for; matrix products, arithmetic and copies ran while one was open for 2% of the time, Pallas kernels for 0%

profile of v4, /device:TPU:0, one launch (start us, length us, event | category | flops | bytes accessed | tf_op | source)
XLA Modules:
  0.0 187.4 jit_solution(5396127582933932212)
XLA Ops:
  0.6 0.0 copy-start
  0.6 0.0 copy-start.4
  0.7 0.9 fusion.3
  1.5 0.2 convolution_convert_fusion.2
  1.7 0.1 copy.28
  1.9 0.1 copy.29
  2.1 0.1 eq.55
  2.1 0.7 convert_element_type.71
  2.9 0.1 copy.30
  3.0 0.1 fusion.6
  3.1 0.0 copy-done
  3.1 0.0 copy-done.4
  3.1 0.0 copy-start.7
  3.1 1.1 copy-done.7
  4.2 0.0 copy-start.8
  4.2 1.1 copy-done.8
  5.4 0.0 copy-start.9
  5.4 1.1 copy-done.9
  6.5 77.6 %shard_map.118 = (bf16[4,256,1408]{2,1,0:T(8,128)(2,1)S(1)}, bf16[4,256,1408]{2,1,0:T(8,128)(2,1)S(1)}, bf16[4,256,1408]{2,1,0:T(8,128)(2,1)S(1)}, bf16[2,4,48,1...) custom-call(bf16[256,1408]{1,0:T(8,128)(2,1)S(1)} %bitcast.48, bf16[256,1408]{1,0:T(8,128)(2,1)S(1)} %bitcast.49, ...), custom_call_target="tpu_custom_call" | custom-call | tf_op jit(solution)/shard_map/pallas_call | solution.py:137
  84.1 0.0 copy-start.2
  84.1 0.0 copy-start.1
  84.1 0.0 copy-start.5
  84.1 0.0 copy-start.3
  84.1 0.0 copy-start.6
  84.2 1.4 fusion.8
  85.5 0.2 copy-done.2
  85.7 0.0 copy-start.10
  85.7 1.5 slice.174
  87.2 0.0 collective-permute-start.1
  87.2 0.0 copy-done.1
  87.2 1.4 fusion.7
  88.6 0.0 copy-done.5
  88.6 0.0 copy-done.10
  88.6 0.0 copy-start.12
  88.6 0.9 slice.175
  89.6 0.5 collective-permute-start
  90.1 0.0 copy-done.3
  90.1 0.0 copy-done.6
  90.1 0.0 copy-start.11
  90.1 1.4 fusion.9
  91.5 0.0 copy-done.12
  91.5 0.0 copy-start.13
  91.5 1.0 slice.173
  92.4 0.6 copy-done.13
  93.1 0.0 collective-permute-start.2
  93.1 0.0 collective-permute-done.1
  93.1 0.0 collective-permute-done
  93.1 2.3 %collective-permute-done.2 = bf16[192,1408]{1,0:T(8,128)(2,1)} collective-permute-done((bf16[192,1408]{1,0:T(8,128)(2,1)}, bf16[192,1408]{1,0:T(8,128)(2,1)}, u32[]{:S(2)}, u32[]{:S(2)}) %collective-permute-start.2) | collective-permute-done | bytes 540704 | tf_op jit(solution)/shard_map/ppermute | solution.py:291
  95.4 0.0 copy-done.11
  95.4 2.8 %multiply_convert_fusion = (bf16[192,1408]{1,0:T(8,128)(2,1)S(1)}, bf16[192,1408]{1,0:T(8,128)(2,1)S(1)}, bf16[192,1408]{1,0:T(8,128)(2,1)S(1)}) fusion(bf16[192,1408]{1,0:T(8,128)(2,1)} %collective-permute-done.2, f32[384,1408]{1,0:T(8,128)} %copy-done.13, bf16[192,1408]{1,0:T(8,128)(2,1)} %collective-permute-done, f32[384,1408]{1,0:T(8,128)} %copy-done.12, ...), kind=kLoop, calls=%fused_computation.12 | loop fusion | flops 5947392 | bytes 6488064 | tf_op jit(solution)/shard_map/convert_element_type | solution.py:359
  98.1 79.8 %shard_map.119 = (bf16[256,1408]{1,0:T(8,128)(2,1)S(1)}, bf16[256,1408]{1,0:T(8,128)(2,1)S(1)}, bf16[256,1408]{1,0:T(8,128)(2,1)S(1)}, bf16[256,1408]{1,0:T(8,12...) custom-call(bf16[384,1024]{1,0:T(8,128)(2,1)} %bitcast.45, ...), custom_call_target="tpu_custom_call" | custom-call | tf_op jit(solution)/shard_map/pallas_call | solution.py:228
  177.9 1.5 broadcast_select_fusion
  179.6 1.4 convolution_convert_fusion.1
  181.0 0.5 fusion.10
  181.6 0.0 copy-start.16
  181.7 1.4 convolution_convert_fusion
  183.1 0.1 select_reduce_fusion
  183.1 0.6 select_reduce_fusion.1
  183.8 0.0 copy-done.16
  183.8 0.0 copy-start.14
  183.8 1.4 add_bitcast_fusion.2
  185.2 0.0 copy-done.14
  185.2 0.1 copy-done.15
  185.3 2.0 %add_bitcast_fusion = (f32[1,256,1408]{2,1,0:T(8,128)}, f32[1,256,1408]{2,1,0:T(8,128)}) fusion(bf16[256,1408]{1,0:T(8,128)(2,1)S(1)} %copy-done.14, bf16[256,1408]{1,0:T(8,128)(2,1)S(1)} %get-tuple-element.36, bf16[256,1408]{1,0:T(8,128)(2,1)S(1)} %get-tuple-element.35, bf16[256,1408]{1,0:T(8,128)(2,1)S(1)} %copy-done.15, ...), kind=kLoop, calls=%fused_computation.2 | loop fusion | flops 3604480 | bytes 7208960 | tf_op jit(solution)/shard_map/broadcast_in_dim | solution.py:370
  (24 shorter events, 0.4 us)
Async XLA Ops:
  0.6 2.5 %copy-start = (bf16[256,2048]{1,0:T(8,128)(2,1)S(1)}, bf16[256,2048]{1,0:T(8,128)(2,1)}, u32[]{:S(2)}) copy-start(bf16[256,2048]{1,0:T(8,128)(2,1)} %refs_6_.1) | copy-start | bytes 3145732
  0.6 2.5 %copy-start.4 = (bf16[256,2048]{1,0:T(8,128)(2,1)S(1)}, bf16[256,2048]{1,0:T(8,128)(2,1)}, u32[]{:S(2)}) copy-start(bf16[256,2048]{1,0:T(8,128)(2,1)} %refs_5_.1) | copy-start | bytes 3145732
  3.1 1.1 copy-start.7
  4.2 1.1 copy-start.8
  5.4 1.1 copy-start.9
  84.1 1.6 copy-start.2
  84.1 3.1 %copy-start.1 = (bf16[4,256,1408]{2,1,0:T(8,128)(2,1)}, bf16[4,256,1408]{2,1,0:T(8,128)(2,1)S(1)}, u32[]{:S(2)}) copy-start(bf16[4,256,1408]{2,1,0:T(8,128)(2,1)S(1)} %get-tuple-element.24) | copy-start | bytes 8650756
  84.1 4.5 %copy-start.5 = (bf16[2,4,48,1024]{3,2,1,0:T(8,128)(2,1)}, bf16[2,4,48,1024]{3,2,1,0:T(8,128)(2,1)S(1)}, u32[]{:S(2)}) copy-start(bf16[2,4,48,1024]{3,2,1,0:T(8,128)(2,1)S(1)} %get-tuple-element.22) | copy-start | bytes 2359300
  84.1 5.9 %copy-start.3 = (bf16[4,256,1408]{2,1,0:T(8,128)(2,1)}, bf16[4,256,1408]{2,1,0:T(8,128)(2,1)S(1)}, u32[]{:S(2)}) copy-start(bf16[4,256,1408]{2,1,0:T(8,128)(2,1)S(1)} %get-tuple-element.26) | copy-start | bytes 8650756
  84.1 5.9 %copy-start.6 = (bf16[2,4,48,1024]{3,2,1,0:T(8,128)(2,1)}, bf16[2,4,48,1024]{3,2,1,0:T(8,128)(2,1)S(1)}, u32[]{:S(2)}) copy-start(bf16[2,4,48,1024]{3,2,1,0:T(8,128)(2,1)S(1)} %get-tuple-element.23) | copy-start | bytes 2359300
  85.7 2.9 %copy-start.10 = (f32[384,1408]{1,0:T(8,128)}, f32[384,1408]{1,0:T(8,128)S(1)}, u32[]{:S(2)}) copy-start(f32[384,1408]{1,0:T(8,128)S(1)} %fusion.8) | copy-start | bytes 6488068
  87.2 5.9 %collective-permute-start.1 = (bf16[192,1408]{1,0:T(8,128)(2,1)}, bf16[192,1408]{1,0:T(8,128)(2,1)}, u32[]{:S(2)}, u32[]{:S(2)}) collective-permute-start(bf16[192,1408]{1,0:T(8,128)(2,1)} %slice.174), channel_id=1, source_target_pairs={{0,1},{1,0},{2,3},{3,2},{4,5},{5,4},{6,7},{7,6},{8,9},{9,8},{10,11... | collective-permute-start | bytes 1622024 | tf_op jit(solution)/shard_map/ppermute | solution.py:291
  88.6 2.9 %copy-start.12 = (f32[384,1408]{1,0:T(8,128)}, f32[384,1408]{1,0:T(8,128)S(1)}, u32[]{:S(2)}) copy-start(f32[384,1408]{1,0:T(8,128)S(1)} %fusion.7) | copy-start | bytes 6488068
  89.6 3.5 %collective-permute-start = (bf16[192,1408]{1,0:T(8,128)(2,1)}, bf16[192,1408]{1,0:T(8,128)(2,1)}, u32[]{:S(2)}, u32[]{:S(2)}) collective-permute-start(bf16[192,1408]{1,0:T(8,128)(2,1)} %slice.175), channel_id=1, source_target_pairs={{0,1},{1,0},{2,3},{3,2},{4,5},{5,4},{6,7},{7,6},{8,9},{9,8},{10,11... | collective-permute-start | bytes 1622024 | tf_op jit(solution)/shard_map/ppermute | solution.py:291
  90.1 5.3 %copy-start.11 = (f32[384,1408]{1,0:T(8,128)S(1)}, f32[384,1408]{1,0:T(8,128)}, u32[]{:S(2)}) copy-start(f32[384,1408]{1,0:T(8,128)} %copy-done.10) | copy-start | bytes 6488068
  91.5 1.6 copy-start.13
  93.1 2.3 %collective-permute-start.2 = (bf16[192,1408]{1,0:T(8,128)(2,1)}, bf16[192,1408]{1,0:T(8,128)(2,1)}, u32[]{:S(2)}, u32[]{:S(2)}) collective-permute-start(bf16[192,1408]{1,0:T(8,128)(2,1)} %slice.173), channel_id=1, source_target_pairs={{0,1},{1,0},{2,3},{3,2},{4,5},{5,4},{6,7},{7,6},{8,9},{9,8},{10,11... | collective-permute-start | bytes 1622024 | tf_op jit(solution)/shard_map/ppermute | solution.py:291
  181.6 2.2 %copy-start.16 = (bf16[256,1408]{1,0:T(8,128)(2,1)S(1)}, bf16[256,1408]{1,0:T(8,128)(2,1)}, u32[]{:S(2)}) copy-start(bf16[256,1408]{1,0:T(8,128)(2,1)} %get-tuple-element.31) | copy-start | bytes 2162692
  183.8 1.4 copy-start.14
  183.8 1.6 copy-start.15

commit v5 on v4

--- a/solution.py
+++ b/solution.py
@@ -341,18 +341,19 @@
         row_in = jnp.concatenate([row_mine, swap(row_other)], axis=0)
         out_grad = jnp.concatenate([og_mine, swap(og_other)], axis=0)
 
-    def summed(x):
-        return x[:rows] + swap(x[rows:].astype(BF16)).astype(F32)
+    def summed(x, w, dims):
+        theirs = swap(dot(x[rows:], w, dims).astype(BF16))
+        return dot(x[:rows], w, dims) + theirs.astype(F32)
 
     def both(x):
         return jnp.concatenate([x, swap(x)], axis=0)
 
     plain, turned = ((1,), (0,)), ((1,), (1,))
-    gate_pre = summed(dot(row_in, full_gate, plain))
-    up_pre = summed(dot(row_in, full_up, plain))
+    gate_pre = summed(row_in, full_gate, plain)
+    up_pre = summed(row_in, full_up, plain)
     sigmoid_g = jax.nn.sigmoid(gate_pre)
     hidden = (gate_pre * sigmoid_g * up_pre).astype(BF16)
-    hidden_grad = summed(dot(out_grad, full_down, plain))
+    hidden_grad = summed(out_grad, full_down, plain)
     gate_grad = (
         hidden_grad * up_pre * sigmoid_g * (1.0 + gate_pre * (1.0 - sigmoid_g))
     ).astype(BF16)

time: 188 us -> 190 us (1.011)
  matrix products: 7.6 us -> 15.1 us
  other arithmetic: 10.1 us -> 7.16 us
  waiting for transfers between devices: 2.26 us -> 0.01 us
    dot_general x7 -> x10, matrix products: 7.6 us -> 15.1 us  [dot(): return lax.dot_general(a, b, (dims, ((), ())), preferred_element_type=F32)]
    convert_element_type x1 -> x0, other arithmetic: 2.78 us -> none  [on_device(): up_grad = (hidden_grad * gate_pre * sigmoid_g).astype(BF16)]
    unnamed x48 -> x46, local copies, waits for them, and re-layouts: 4.54 us -> 7.19 us
    slice x3 -> x2, local copies, waits for them, and re-layouts: 3.39 us -> 0.89 us  [summed(): theirs = swap(dot(x[rows:], w, dims).astype(BF16))]
    ppermute x3, waiting for transfers between devices: 2.26 us -> 0.01 us  [swap(): return lax.ppermute(x, 'fsdp', pairs)]
  transfers between devices with their start and end apart: 3 -> 3, of which waited for: 1 -> 0; matrix products, arithmetic and copies ran while one was open for 2% -> 4% of each run, Pallas kernels for 0% -> 0%
where the time goes in v5:
time: 190 us
  Pallas kernels  157 us (83%)
  matrix products  15.1 us (8%)
  local copies, waits for them, and re-layouts  8.64 us (5%)
  other arithmetic  7.16 us (4%)
    pallas_call x1, Pallas kernels, scatter_call(): pl.pallas_call(functools.partial(scatter_kernel, groups), out_shape=[jax....  79.7 us
    pallas_call x1, Pallas kernels, gather_call(): pl.pallas_call(functools.partial(gather_kernel, groups, count, n_rows), o...  77.6 us
    dot_general x10, matrix products, dot(): return lax.dot_general(a, b, (dims, ((), ())), preferred_element_type=F32)  15.1 us
    unnamed x46, local copies, waits for them, and re-layouts  7.19 us
  transfers between devices with their start and end apart: 3, of which 0 were waited for; matrix products, arithmetic and copies ran while one was open for 4% of the time, Pallas kernels for 0%

profile of v5, /device:TPU:0, one launch (start us, length us, event | category | flops | bytes accessed | tf_op | source)
XLA Modules:
  0.0 189.8 jit_solution(2996977551765196929)
XLA Ops:
  0.6 0.7 fusion.3
  1.4 0.2 convolution_convert_fusion.5
  1.6 0.1 copy.28
  1.7 0.1 copy.29
  1.9 0.1 eq.55
  2.0 0.7 convert_element_type.77
  2.7 0.1 copy.30
  2.8 0.1 fusion.6
  2.9 0.0 copy-start.4
  3.0 1.2 copy-done.4
  4.2 0.0 copy-start.8
  4.2 1.2 copy-done.8
  5.4 0.0 copy-start.9
  5.4 1.1 copy-done.9
  6.5 0.0 copy-start.10
  6.5 1.1 copy-done.10
  7.6 0.0 copy-start.11
  7.6 1.1 copy-done.11
  8.7 77.6 %shard_map.118 = (bf16[4,256,1408]{2,1,0:T(8,128)(2,1)S(1)}, bf16[4,256,1408]{2,1,0:T(8,128)(2,1)S(1)}, bf16[4,256,1408]{2,1,0:T(8,128)(2,1)S(1)}, bf16[2,4,48,1...) custom-call(bf16[256,1408]{1,0:T(8,128)(2,1)S(1)} %bitcast.58, bf16[256,1408]{1,0:T(8,128)(2,1)S(1)} %bitcast.59, ...), custom_call_target="tpu_custom_call" | custom-call | tf_op jit(solution)/shard_map/pallas_call | solution.py:137
  86.4 0.0 copy-start.1
  86.4 0.0 copy-start.6
  86.4 0.0 copy-start.7
  86.4 0.0 copy-start.2
  86.4 0.0 copy-start
  86.4 0.1 fusion.8
  86.5 2.1 %convolution_convert_fusion.3 = bf16[192,1408]{1,0:T(8,128)(2,1)} fusion(bf16[192,1024]{1,0:T(8,128)(2,1)S(1)} %bitcast.63, bf16[1024,1408]{1,0:T(8,128)(2,1)S(1)} %bitcast.50), kind=kOutput, calls=%fused_computation.3 | convolution fusion | flops 553918464 | bytes 3817472 | tf_op jit(solution)/shard_map/dot_general | solution.py:18
  88.6 0.0 collective-permute-start.1
  88.6 1.9 %convolution_convert_fusion.4 = bf16[192,1408]{1,0:T(8,128)(2,1)} fusion(bf16[192,1024]{1,0:T(8,128)(2,1)S(1)} %bitcast.64, bf16[1024,1408]{1,0:T(8,128)(2,1)S(1)} %bitcast.47), kind=kOutput, calls=%fused_computation.4 | convolution fusion | flops 553918464 | bytes 3817472 | tf_op jit(solution)/shard_map/dot_general | solution.py:18
  90.5 0.0 copy-done.1
  90.5 0.0 copy-done.6
  90.5 0.2 collective-permute-start
  90.7 0.0 copy-done.7
  90.7 0.8 fusion.7
  91.5 0.0 copy-done.2
  91.5 1.6 convolution_convert_fusion.2
  93.1 0.3 collective-permute-start.2
  93.5 2.6 %fusion.10 = f32[192,1408]{1,0:T(8,128)S(1)} fusion(bf16[192,1024]{1,0:T(8,128)(2,1)S(1)} %bitcast.61, bf16[1024,1408]{1,0:T(8,128)(2,1)} %bitcast.51), kind=kOutput, calls=%fused_computation.60 | convolution fusion | flops 553648128 | bytes 4358144 | tf_op jit(solution)/shard_map/dot_general | solution.py:18
  96.1 0.0 copy-done
  96.1 0.0 copy-start.3
  96.1 0.0 copy-start.15
  96.1 0.8 fusion.9
  96.9 0.0 collective-permute-done.1
  96.9 0.0 collective-permute-done
  96.9 0.0 collective-permute-done.2
  96.9 1.0 copy-done.3
  97.9 0.0 copy-done.15
  98.0 2.6 %multiply_convert_fusion = (bf16[192,1408]{1,0:T(8,128)(2,1)S(1)}, bf16[192,1408]{1,0:T(8,128)(2,1)S(1)}, bf16[192,1408]{1,0:T(8,128)(2,1)S(1)}) fusion(bf16[192,1408]{1,0:T(8,128)(2,1)} %collective-permute-done.2, f32[192,1408]{1,0:T(8,128)S(1)} %fusion.9, bf16[192,1408]{1,0:T(8,128)(2,1)} %collective-permute-done, f32[192,1408]{1,0:T(8,128)S(1)} %fusion.10, ...), kind=kOutput, calls=%fused_computation.9 | convolution fusion | flops 559595520 | bytes 8683520 | tf_op jit(solution)/shard_map/dot_general | solution.py:18
  100.5 79.7 %shard_map.119 = (bf16[256,1408]{1,0:T(8,128)(2,1)S(1)}, bf16[256,1408]{1,0:T(8,128)(2,1)S(1)}, bf16[256,1408]{1,0:T(8,128)(2,1)S(1)}, bf16[256,1408]{1,0:T(8,12...) custom-call(bf16[384,1024]{1,0:T(8,128)(2,1)} %bitcast.56, ...), custom_call_target="tpu_custom_call" | custom-call | tf_op jit(solution)/shard_map/pallas_call | solution.py:228
  180.3 1.5 broadcast_select_fusion
  181.8 0.0 copy-start.5
  181.9 1.4 convolution_convert_fusion.1
  183.4 0.0 copy-done.5
  183.4 0.5 fusion.11
  184.0 0.0 copy-start.14
  184.1 1.4 convolution_convert_fusion
  185.5 0.1 select_reduce_fusion
  185.5 0.6 select_reduce_fusion.1
  186.2 0.0 copy-done.14
  186.2 0.0 copy-start.12
  186.2 0.0 copy-start.13
  186.2 1.4 add_bitcast_fusion.2
  187.6 0.0 copy-done.12
  187.6 0.1 copy-done.13
  187.7 2.0 %add_bitcast_fusion = (f32[1,256,1408]{2,1,0:T(8,128)}, f32[1,256,1408]{2,1,0:T(8,128)}) fusion(bf16[256,1408]{1,0:T(8,128)(2,1)S(1)} %copy-done.12, bf16[256,1408]{1,0:T(8,128)(2,1)S(1)} %get-tuple-element.36, bf16[256,1408]{1,0:T(8,128)(2,1)S(1)} %get-tuple-element.35, bf16[256,1408]{1,0:T(8,128)(2,1)S(1)} %copy-done.13, ...), kind=kLoop, calls=%fused_computation.5 | loop fusion | flops 3604480 | bytes 7208960 | tf_op jit(solution)/shard_map/broadcast_in_dim | solution.py:371
  (23 shorter events, 0.4 us)
Async XLA Ops:
  2.9 1.2 copy-start.4
  4.2 1.2 copy-start.8
  5.4 1.1 copy-start.9
  6.5 1.1 copy-start.10
  7.6 1.1 copy-start.11
  86.4 4.2 %copy-start.1 = (bf16[4,256,1408]{2,1,0:T(8,128)(2,1)}, bf16[4,256,1408]{2,1,0:T(8,128)(2,1)S(1)}, u32[]{:S(2)}) copy-start(bf16[4,256,1408]{2,1,0:T(8,128)(2,1)S(1)} %get-tuple-element.25) | copy-start | bytes 8650756
  86.4 4.2 %copy-start.6 = (bf16[2,4,48,1024]{3,2,1,0:T(8,128)(2,1)}, bf16[2,4,48,1024]{3,2,1,0:T(8,128)(2,1)S(1)}, u32[]{:S(2)}) copy-start(bf16[2,4,48,1024]{3,2,1,0:T(8,128)(2,1)S(1)} %get-tuple-element.22) | copy-start | bytes 2359300
  86.4 4.3 %copy-start.7 = (bf16[2,4,48,1024]{3,2,1,0:T(8,128)(2,1)}, bf16[2,4,48,1024]{3,2,1,0:T(8,128)(2,1)S(1)}, u32[]{:S(2)}) copy-start(bf16[2,4,48,1024]{3,2,1,0:T(8,128)(2,1)S(1)} %get-tuple-element.23) | copy-start | bytes 2359300
  86.4 5.1 %copy-start.2 = (bf16[4,256,1408]{2,1,0:T(8,128)(2,1)}, bf16[4,256,1408]{2,1,0:T(8,128)(2,1)S(1)}, u32[]{:S(2)}) copy-start(bf16[4,256,1408]{2,1,0:T(8,128)(2,1)S(1)} %get-tuple-element.26) | copy-start | bytes 8650756
  86.4 9.7 %copy-start = (bf16[4,256,1408]{2,1,0:T(8,128)(2,1)}, bf16[4,256,1408]{2,1,0:T(8,128)(2,1)S(1)}, u32[]{:S(2)}) copy-start(bf16[4,256,1408]{2,1,0:T(8,128)(2,1)S(1)} %get-tuple-element.24) | copy-start | bytes 8650756
  88.6 8.3 %collective-permute-start.1 = (bf16[192,1408]{1,0:T(8,128)(2,1)}, bf16[192,1408]{1,0:T(8,128)(2,1)}, u32[]{:S(2)}, u32[]{:S(2)}) collective-permute-start(bf16[192,1408]{1,0:T(8,128)(2,1)} %convolution_convert_fusion.3), channel_id=1, source_target_pairs={{0,1},{1,0},{2,3},{3,2},{4,5},{5,4},{6,7},{7,6},{8,9},{9,8},{10,11... | collective-permute-start | bytes 1622024 | tf_op jit(solution)/shard_map/ppermute | solution.py:291
  90.5 6.4 %collective-permute-start = (bf16[192,1408]{1,0:T(8,128)(2,1)}, bf16[192,1408]{1,0:T(8,128)(2,1)}, u32[]{:S(2)}, u32[]{:S(2)}) collective-permute-start(bf16[192,1408]{1,0:T(8,128)(2,1)} %convolution_convert_fusion.4), channel_id=1, source_target_pairs={{0,1},{1,0},{2,3},{3,2},{4,5},{5,4},{6,7},{7,6},{8,9},{9,8},{10,11... | collective-permute-start | bytes 1622024 | tf_op jit(solution)/shard_map/ppermute | solution.py:291
  93.1 3.8 %collective-permute-start.2 = (bf16[192,1408]{1,0:T(8,128)(2,1)}, bf16[192,1408]{1,0:T(8,128)(2,1)}, u32[]{:S(2)}, u32[]{:S(2)}) collective-permute-start(bf16[192,1408]{1,0:T(8,128)(2,1)} %convolution_convert_fusion.2), channel_id=1, source_target_pairs={{0,1},{1,0},{2,3},{3,2},{4,5},{5,4},{6,7},{7,6},{8,9},{9,8},{10,11... | collective-permute-start | bytes 1622024 | tf_op jit(solution)/shard_map/ppermute | solution.py:291
  96.1 1.8 copy-start.3
  96.1 1.9 copy-start.15
  181.8 1.5 copy-start.5
  184.0 2.2 %copy-start.14 = (bf16[256,1408]{1,0:T(8,128)(2,1)S(1)}, bf16[256,1408]{1,0:T(8,128)(2,1)}, u32[]{:S(2)}) copy-start(bf16[256,1408]{1,0:T(8,128)(2,1)} %get-tuple-element.31) | copy-start | bytes 2162692
  186.2 1.4 copy-start.12
  186.2 1.6 copy-start.13
